TPU v7x, 128 devices: a whole 4x4x4 slice. The times are simulated.
128 devices in a mesh: orient: 8 (over z, y_lo), frame: 16 (over x, y_hi, core).
Axes of the slice: x: 4, y: 4 (y_hi: 2, y_lo: 2; y = y_hi * 2 + y_lo), z: 4, core: 2. Of those that a mesh axis runs over, the one named last changes fastest.
Arguments:
- slices: float32 [512, 2048], P('orient', 'frame'), may hold values from 0.2 to 5
- counts: float32 [8192, 2048], P('frame'), may hold values from 0 to 600, as said below
- fluence: float32 [8192], P('frame'), may hold values from 0.5 to 2
- tile_brick: int32 [16, 512, 1], P('frame', 'orient'), may hold values from 0 to 127; in each aligned block of 64 rows (0 to 63, 64 to 127, ..., all dimensions but the last counted through in order) at most 4 rows name the same one
- tile_base: int32 [16, 512], P('frame', 'orient'), may hold values from 0 to 896
Outputs:
- new_slices: float32 [512, 2048], P('orient', 'frame')
- intensity: float32 [128, 1024], P(('orient', 'frame'))
Inputs may be any that keep to these rules, and one draw needn't show every extreme that they name: `tile_brick`: in each aligned block of 64 rows (one tile of each of one index of orient's orientations) no brick is named more than 4 times. `counts`: whole numbers.
All inputs are finite; a program needn't handle non-finite values.
Results may differ from a plain program's by a relative error of at most 0.0003.
Values sent between devices are 32-bit elements; how exact they have to be, the bound alone decides.
A program may use at most 64 MiB of HBM per device.

v0:
```python
import jax
import jax.numpy as jnp
from jax import lax
from jax.sharding import PartitionSpec as P

VOX_DEV = 1024
ITERS = 2


BACKGROUND = 0.1
SHARPNESS = 0.02


def skew_sum(block, voxels):
    width = block.shape[1]
    spread = jnp.pad(block.T, ((0, 0), (0, voxels + 1 - block.shape[0])))
    return jnp.sum(spread.reshape(-1)[: width * voxels].reshape(width, voxels), axis=0)


def windows_of(intensity, width, starts):
    voxels = intensity.shape[0]
    repeated = jnp.broadcast_to(intensity[None, :], (width, voxels)).reshape(-1)
    repeated = jnp.pad(repeated, (0, width)).reshape(width, voxels + 1)
    return repeated[:, :starts].T


def on_device(slices, counts, fluence, tile_brick, tile_base):
    rows = slices.shape[0]
    width = slices.shape[1]
    columns = tile_brick.shape[0]
    tile = width // columns
    bricks = lax.axis_size("orient") * lax.axis_size("frame")
    voxels = VOX_DEV
    starts = voxels - tile + 1
    capacity = max(4, 2 * rows // bricks)
    highest = lax.Precision.HIGHEST
    brick = tile_brick[:, :, 0]
    onehot = (brick[:, :, None] == jnp.arange(bricks, dtype=jnp.int32)[None, None, :]).astype(
        jnp.int32
    )
    before = jnp.cumsum(onehot, axis=1) - onehot
    slot = jnp.sum(before * onehot, axis=2)
    column_ids = jnp.broadcast_to(jnp.arange(columns, dtype=jnp.int32)[:, None], brick.shape)
    bases = (
        jnp.full((bricks, columns, capacity), -1, jnp.int32)
        .at[brick, column_ids, slot]
        .set(tile_base)
    )
    place = (
        (brick[:, :, None, None] == jnp.arange(bricks, dtype=jnp.int32)[None, None, :, None])
        & (slot[:, :, None, None] == jnp.arange(capacity, dtype=jnp.int32)[None, None, None, :])
    ).astype(jnp.float32)
    start_ids = jnp.arange(starts, dtype=jnp.int32)
    local = slices
    intensity = jnp.zeros((voxels,), jnp.float32)
    hits = jnp.ones((voxels,), jnp.float32)
    for turn in range(ITERS):
        piece = lax.all_gather(local, "frame", axis=1, tiled=True)
        like_sum = lax.dot_general(
            jnp.log(piece + BACKGROUND),
            counts,
            (((1,), (1,)), ((), ())),
            precision=highest,
            preferred_element_type=jnp.float32,
        )
        total = jnp.sum(piece, axis=1)
        score = SHARPNESS * (like_sum - total[:, None] * fluence[None, :])
        top = jnp.max(score, axis=0)
        peak = lax.pmax(top, "orient")
        expo = jnp.exp(score - peak[None, :])
        norm = lax.psum(jnp.sum(expo, axis=0), "orient")
        prob = expo / norm[None, :]
        share = lax.psum_scatter(
            lax.dot_general(
                counts,
                prob,
                (((0,), (1,)), ((), ())),
                precision=highest,
                preferred_element_type=jnp.float32,
            ),
            "frame",
            scatter_dimension=0,
            tiled=True,
        )
        weight = lax.psum(jnp.dot(prob, fluence, precision=highest), "frame")
        updated = (share.T + local) / (weight + 1.0)[:, None]
        tiles = updated.reshape(rows, columns, tile).transpose(1, 0, 2)
        values = jnp.einsum("crbk,crt->bckt", place, tiles, precision=highest)
        got_values, got_bases = (
            lax.all_to_all(values, ("orient", "frame"), split_axis=0, concat_axis=0, tiled=True),
            lax.all_to_all(bases, ("orient", "frame"), split_axis=0, concat_axis=0, tiled=True),
        )
        flat_base = got_bases.reshape(-1)
        selector = (flat_base[:, None] == start_ids[None, :]).astype(jnp.float32)
        flat_values = got_values.reshape(-1, tile)
        sums = skew_sum(jnp.dot(selector.T, flat_values, precision=highest), voxels)
        if turn == 0:
            counted = jnp.sum(selector, axis=0)
            hits = skew_sum(jnp.broadcast_to(counted[:, None], (starts, tile)), voxels)
        intensity = sums / jnp.maximum(hits, 1.0)
        looked = jnp.dot(selector, windows_of(intensity, tile, starts), precision=highest).reshape(
            got_values.shape
        )
        returned = lax.all_to_all(
            looked, ("orient", "frame"), split_axis=0, concat_axis=0, tiled=True
        )
        local_tiles = jnp.einsum("crbk,bckt->crt", place, returned, precision=highest)
        local = local_tiles.transpose(1, 0, 2).reshape(rows, width)
    return (local, intensity[None, :])


def solution(mesh):
    in_specs = (
        P("orient", "frame"),
        P("frame", None),
        P("frame"),
        P("frame", "orient", None),
        P("frame", "orient"),
    )
    out_specs = (P("orient", "frame"), P(("orient", "frame"), None))
    return jax.shard_map(
        on_device, mesh=mesh, in_specs=in_specs, out_specs=out_specs, check_vma=False
    )
```

profile of v0, /device:TPU:1, one launch (start us, length us, event | category | flops | bytes accessed | tf_op | source)
XLA Modules:
  0.0 358.5 jit_solution(3558878496337462783)
XLA Ops:
  7.2 0.0 reduce-scatter.3.cloned.1.call-start
  7.2 27.3 %all_gather.6 = f32[64,2048]{1,0:T(8,128)S(1)} all-gather(f32[64,128]{1,0:T(8,128)} %param.5), channel_id=1, replica_groups=mesh['orient'=8,'frame'=16] {'frame'}, dimensions={1}, use_global_device_ids=true | all-gather | bytes 557056 | tf_op jit(solution)/shard_map/all_gather | solution.py:58
  34.6 0.1 reduce_sum.85
  34.7 0.0 copy-start.4
  34.7 6.3 %fusion.58 = (f32[512]{0:T(512)S(1)}, f32[64,512]{1,0:T(8,128)S(1)}) fusion(f32[512]{0:T(512)} %param.7, f32[64]{0:T(128)S(1)} %reduce_sum.85, f32[512,2048]{1,0:T(8,128)} %param.6, f32[64,2048]{1,0:T(8,128)S(1)} %all_gather.6), kind=kOutput, calls=%fused_computation.85 | convolution fusion | flops 805568000 | bytes 4854016 | tf_op jit(solution)/shard_map/dot_general | solution.py:59
  41.0 0.0 copy-start.2
  41.1 0.0 copy-start
  41.1 16.5 %pmax.14 = f32[512]{0:T(512)S(1)} all-reduce(f32[512]{0:T(512)S(1)} %get-tuple-element.2), channel_id=1, replica_groups=mesh['orient'=8,'frame'=16] {'orient'}, use_global_device_ids=true, to_apply=%region_5.6 | all-reduce | flops 512 | bytes 4096 | tf_op jit(solution)/shard_map/pmax | solution.py:69
  57.6 12.6 %psum.28 = f32[512]{0:T(512)S(1)} all-reduce(f32[512]{0:T(512)S(1)} %fusion.30), channel_id=1, replica_groups=mesh['orient'=8,'frame'=16] {'orient'}, use_global_device_ids=true, to_apply=%region_7.8 | all-reduce | flops 512 | bytes 4096 | tf_op jit(solution)/shard_map/psum | solution.py:71
  70.2 5.6 %convolution_bitcast_fusion.1 = f32[2048,64]{0,1:T(8,128)} fusion(f32[512,2048]{1,0:T(8,128)} %param.6, f32[64,512]{1,0:T(8,128)S(1)} %get-tuple-element.3, f32[512]{0:T(512)S(1)} %psum.28, f32[512]{0:T(512)S(1)} %pmax.14), kind=kOutput, calls=%fused_computation.2 | convolution fusion | flops 805371904 | bytes 4853760 | tf_op jit(solution)/shard_map/dot_general | solution.py:74
  75.8 0.0 reduce-scatter.3.cloned.1.call-update
  75.8 0.1 fusion.51
  75.9 0.1 reduce_window_sum.11
  76.0 0.2 select_reduce_fusion
  76.3 3.5 scatter_fusion
  79.7 0.7 copy.25
  80.5 10.8 %all-to-all-start = ((s32[128,1,4]{2,1,0:T(1,128)}), s32[128,1,4]{2,1,0:T(1,128)S(1)}, u32[]{:S(2)}, u32[]{:S(2)}) async-start(s32[128,1,4]{2,1,0:T(1,128)} %copy.25), calls=%async_computation | async-start | bytes 131072 | tf_op jit(solution)/shard_map/all_to_all | solution.py:91
  91.3 0.0 copy-done.2
  91.3 0.2 convolution_bitcast_fusion.7
  91.5 33.8 %psum.29 = f32[64]{0:T(128)S(1)} all-reduce(f32[64]{0:T(128)S(1)} %convolution_bitcast_fusion.7), channel_id=1, replica_groups=mesh['orient'=8,'frame'=16] {'frame'}, use_global_device_ids=true, to_apply=%region_9.10 | all-reduce | flops 64 | bytes 512 | tf_op jit(solution)/shard_map/psum | solution.py:85
  125.3 0.1 iota_compare_fusion.4
  125.3 16.4 %reduce-scatter.3.cloned.1.call-done = f32[128,64]{0,1:T(8,128)} async-done(((f32[2048,64]{0,1:T(8,128)}), f32[128,64]{0,1:T(8,128)}) %reduce-scatter.3.cloned.1.call-update) | async-done | bytes 32784 | tf_op jit(solution)/shard_map/reduce_scatter | solution.py:73
  141.8 1.1 convolution_bitcast_fusion.3
  142.9 0.8 copy.26
  143.7 0.0 all-to-all-done
  143.7 9.4 %all-to-all-start.1 = ((f32[128,1,4,128]{3,2,1,0:T(4,128)}), f32[128,1,4,128]{3,2,1,0:T(4,128)S(1)}, u32[]{:S(2)}, u32[]{:S(2)}) async-start(f32[128,1,4,128]{3,2,1,0:T(4,128)} %copy.26), calls=%async_computation.2 | async-start | bytes 524288 | tf_op jit(solution)/shard_map/all_to_all | solution.py:90
  153.1 0.2 reduce-scatter.5.cloned.1.call-start
  153.3 0.5 broadcast.219
  153.9 0.8 reduce.4
  154.7 0.1 eq.95
  154.8 0.3 convert_reduce_fusion
  155.1 0.3 reshape.278
  155.5 0.1 reshape.279
  155.6 8.4 %all-to-all-done.1 = f32[128,1,4,128]{3,2,1,0:T(4,128)S(1)} async-done(((f32[128,1,4,128]{3,2,1,0:T(4,128)}), f32[128,1,4,128]{3,2,1,0:T(4,128)S(1)}, u32[]{:S(2)}, u32[]{:S(2)}) %all-to-all-start.1) | async-done | bytes 262176 | tf_op jit(solution)/shard_map/all_to_all | solution.py:90
  164.0 1.1 fusion.2
  165.2 0.3 reshape.276
  165.6 0.1 reshape.277
  165.8 0.1 copy.36
  166.0 0.4 reshape.281
  166.4 1.3 fusion.3
  167.7 15.0 %all_to_all.26 = f32[128,1,4,128]{3,2,1,0:T(4,128)S(1)} all-to-all(f32[128,1,4,128]{3,2,1,0:T(4,128)S(1)} %bitcast.85), channel_id=1, replica_groups=mesh['orient'=8,'frame'=16] {'orient','frame'}, dimensions={0} | all-to-all | bytes 524288 | tf_op jit(solution)/shard_map/all_to_all | solution.py:104
  182.7 0.3 convolution_bitcast_fusion.5
  183.0 22.5 %all_gather.7 = f32[64,2048]{1,0:T(8,128)S(1)} all-gather(f32[64,128]{1,0:T(8,128)S(1)} %convolution_bitcast_fusion.5), channel_id=1, replica_groups=mesh['orient'=8,'frame'=16] {'frame'}, dimensions={1}, use_global_device_ids=true | all-gather | bytes 557056 | tf_op jit(solution)/shard_map/all_gather | solution.py:58
  205.5 0.1 reduce_sum.90
  205.6 6.3 %fusion.59 = (f32[512]{0:T(512)S(1)}, f32[64,512]{1,0:T(8,128)S(1)}) fusion(f32[512]{0:T(512)S(1)} %copy-done.2, f32[64]{0:T(128)S(1)} %reduce_sum.90, f32[512,2048]{1,0:T(8,128)} %param.6, f32[64,2048]{1,0:T(8,128)S(1)} %all_gather.7), kind=kOutput, calls=%fused_computation.86 | convolution fusion | flops 805568000 | bytes 4854016 | tf_op jit(solution)/shard_map/dot_general | solution.py:59
  211.9 13.6 %pmax.15 = f32[512]{0:T(512)S(1)} all-reduce(f32[512]{0:T(512)S(1)} %get-tuple-element.4), channel_id=1, replica_groups=mesh['orient'=8,'frame'=16] {'orient'}, use_global_device_ids=true, to_apply=%region_15.16 | all-reduce | flops 512 | bytes 4096 | tf_op jit(solution)/shard_map/pmax | solution.py:69
  225.6 13.3 %psum.30 = f32[512]{0:T(512)S(1)} all-reduce(f32[512]{0:T(512)S(1)} %fusion.32), channel_id=1, replica_groups=mesh['orient'=8,'frame'=16] {'orient'}, use_global_device_ids=true, to_apply=%region_17.18 | all-reduce | flops 512 | bytes 4096 | tf_op jit(solution)/shard_map/psum | solution.py:71
  238.8 5.6 %convolution_bitcast_fusion = f32[2048,64]{0,1:T(8,128)} fusion(f32[512,2048]{1,0:T(8,128)} %param.6, f32[64,512]{1,0:T(8,128)S(1)} %get-tuple-element.5, f32[512]{0:T(512)S(1)} %psum.30, f32[512]{0:T(512)S(1)} %pmax.15), kind=kOutput, calls=%fused_computation.1 | convolution fusion | flops 805371904 | bytes 4853760 | tf_op jit(solution)/shard_map/dot_general | solution.py:74
  244.5 0.0 reduce-scatter.5.cloned.1.call-update
  244.5 0.2 convolution_bitcast_fusion.6
  244.7 40.0 %psum.31 = f32[64]{0:T(128)S(1)} all-reduce(f32[64]{0:T(128)S(1)} %convolution_bitcast_fusion.6), channel_id=1, replica_groups=mesh['orient'=8,'frame'=16] {'frame'}, use_global_device_ids=true, to_apply=%region_19.20 | all-reduce | flops 64 | bytes 512 | tf_op jit(solution)/shard_map/psum | solution.py:85
  284.7 26.1 %reduce-scatter.5.cloned.1.call-done = f32[128,64]{0,1:T(8,128)} async-done(((f32[2048,64]{0,1:T(8,128)}), f32[128,64]{0,1:T(8,128)}) %reduce-scatter.5.cloned.1.call-update) | async-done | bytes 32784 | tf_op jit(solution)/shard_map/reduce_scatter | solution.py:73
  310.8 1.1 convolution_bitcast_fusion.2
  311.9 0.1 copy.30
  312.1 20.1 %all_to_all.27 = f32[128,1,4,128]{3,2,1,0:T(4,128)S(1)} all-to-all(f32[128,1,4,128]{3,2,1,0:T(4,128)S(1)} %copy.30), channel_id=1, replica_groups=mesh['orient'=8,'frame'=16] {'orient','frame'}, dimensions={0} | all-to-all | bytes 524288 | tf_op jit(solution)/shard_map/all_to_all | solution.py:90
  332.2 1.1 fusion
  333.4 0.3 reshape.285
  333.8 0.1 reshape.286
  333.9 0.0 copy-start.1
  334.0 0.1 copy.37
  334.1 0.4 reshape.288
  334.6 1.3 fusion.5
  335.9 15.0 %all_to_all.28 = f32[128,1,4,128]{3,2,1,0:T(4,128)S(1)} all-to-all(f32[128,1,4,128]{3,2,1,0:T(4,128)S(1)} %bitcast.84), channel_id=1, replica_groups=mesh['orient'=8,'frame'=16] {'orient','frame'}, dimensions={0} | all-to-all | bytes 524288 | tf_op jit(solution)/shard_map/all_to_all | solution.py:104
  350.8 0.9 convolution_bitcast_fusion.4
  (31 shorter events, 0.7 us)
Async XLA Ops:
  7.2 134.6 %reduce-scatter.3.cloned.1.call-start = ((), (), s32[]{:S(2)}) async-start(), calls=%async_computation.7 | async-start | bytes 557056 | tf_op jit(solution)/shard_map/reduce_scatter | solution.py:73
  34.7 41.1 %copy-start.3 = (s32[1,64,1]{1,2,0:T(1,128)S(1)}, s32[1,64,1]{1,2,0:T(1,128)}, u32[]{:S(2)}) copy-start(s32[1,64,1]{1,2,0:T(1,128)} %param.8) | copy-start | bytes 772
  34.7 41.6 %copy-start.4 = (s32[1,64]{1,0:T(1,128)S(1)}, s32[1,64]{1,0:T(1,128)}, u32[]{:S(2)}) copy-start(s32[1,64]{1,0:T(1,128)} %param.9) | copy-start | bytes 772
  41.0 50.2 %copy-start.2 = (f32[512]{0:T(512)S(1)}, f32[512]{0:T(512)}, u32[]{:S(2)}) copy-start(f32[512]{0:T(512)} %param.7) | copy-start | bytes 6148
  41.1 100.7 %copy-start = (f32[64,128]{1,0:T(8,128)S(1)}, f32[64,128]{1,0:T(8,128)}, u32[]{:S(2)}) copy-start(f32[64,128]{1,0:T(8,128)} %param.5) | copy-start | bytes 98308
  80.5 63.3 %all-to-all-start = ((s32[128,1,4]{2,1,0:T(1,128)}), s32[128,1,4]{2,1,0:T(1,128)S(1)}, u32[]{:S(2)}, u32[]{:S(2)}) async-start(s32[128,1,4]{2,1,0:T(1,128)} %copy.25), calls=%async_computation | async-start | bytes 131072 | tf_op jit(solution)/shard_map/all_to_all | solution.py:91
  143.7 20.3 %all-to-all-start.1 = ((f32[128,1,4,128]{3,2,1,0:T(4,128)}), f32[128,1,4,128]{3,2,1,0:T(4,128)S(1)}, u32[]{:S(2)}, u32[]{:S(2)}) async-start(f32[128,1,4,128]{3,2,1,0:T(4,128)} %copy.26), calls=%async_computation.2 | async-start | bytes 524288 | tf_op jit(solution)/shard_map/all_to_all | solution.py:90
  153.1 157.7 %reduce-scatter.5.cloned.1.call-start = ((), (), s32[]{:S(2)}) async-start(), calls=%async_computation.8 | async-start | bytes 557056 | tf_op jit(solution)/shard_map/reduce_scatter | solution.py:73
  333.9 17.8 %copy-start.1 = (f32[1024]{0:T(1024)}, f32[1024]{0:T(1024)S(1)}, u32[]{:S(2)}) copy-start(f32[1024]{0:T(1024)S(1)} %maximum_divide_fusion) | copy-start | bytes 12292
Sparse Core Ops, SparseCore 0:
  75.9 65.7 reduce-scatter.2
  244.6 66.1 reduce-scatter.4
where the time goes:
time: 359 us
  blocking collectives  230 us (64%)
  waiting for transfers between devices  50.9 us (14%)
  matrix products  32.6 us (9%)
  starting transfers between devices  20.4 us (6%)
  between operations  14.4 us (4%)
  local copies, waits for them, and re-layouts  8.55 us (2%)
    psum x2, blocking collectives, on_device(): weight = lax.psum(jnp.dot(prob, fluence, precision=highest), 'frame')  73.8 us
    all_gather x2, blocking collectives, on_device(): piece = lax.all_gather(local, 'frame', axis=1, tiled=True)  49.9 us
    reduce_scatter x2, waiting for transfers between devices, on_device(): lax.psum_scatter(lax.dot_general(counts, prob, (((0,), (1,)), ((), ())),...  42.5 us
    pmax x2, blocking collectives, on_device(): peak = lax.pmax(top, 'orient')  30.1 us
    all_to_all x2, blocking collectives, on_device(): lax.all_to_all(looked, ('orient', 'frame'), split_axis=0, concat_axis=0,...  29.9 us
    psum x2, blocking collectives, on_device(): norm = lax.psum(jnp.sum(expo, axis=0), 'orient')  25.8 us
    all_to_all x1, blocking collectives, on_device(): lax.all_to_all(values, ('orient', 'frame'), split_axis=0, concat_axis=0,...  20.1 us
    dot_general x2, matrix products, on_device(): lax.dot_general(jnp.log(piece + BACKGROUND), counts, (((1,), (1,)), ((),...  12.6 us
  transfers between devices with their start and end apart: 4, of which 3 were waited for; matrix products, arithmetic and copies ran while one was open for 3% of the time, Pallas kernels for 0%

commit v1 on v0

v1 whole, which is shorter than its diff:
```python
import functools

import jax
import jax.numpy as jnp
from jax import lax
from jax.experimental import pallas as pl
from jax.experimental.pallas import tpu as pltpu
from jax.sharding import PartitionSpec as P

VOX = 1024
TILE = 128
SUB = VOX // TILE
ITERS = 2
BACKGROUND = 0.1
SHARPNESS = 0.02
MESH = pl.DeviceIdType.MESH
F32 = jnp.float32
BF16 = jnp.bfloat16
LOAD = 4


def split2(x):
    high = x.astype(BF16)
    return high, (x - high.astype(F32)).astype(BF16)


def split3(x):
    high = x.astype(BF16)
    rest = x - high.astype(F32)
    mid = rest.astype(BF16)
    return high, mid, (rest - mid.astype(F32)).astype(BF16)


def iota(shape, axis):
    return lax.broadcasted_iota(jnp.int32, shape, axis)


def kernel(
    n_o,
    n_f,
    slices_ref,
    codes_ref,
    fluence_ref,
    counts_ref,
    new_ref,
    out_ref,
    raw,
    count_high,
    count_low,
    held,
    codes,
    stats,
    dens,
    gather_to,
    gather_from,
    shifts,
    tiles,
    marks,
    logs,
    part_out,
    part_in,
    brick_out,
    brick_in,
    volume,
    spread,
    hits_out,
    hits_in,
    load_sem,
    frame_send,
    frame_recv,
    orient_send,
    orient_recv,
):
    o = lax.axis_index("orient")
    f = lax.axis_index("frame")
    rows = slices_ref.shape[0]
    frames = counts_ref.shape[0]
    pair = 2 * rows
    block = n_f * SUB
    chunks = frames // TILE

    barrier = pltpu.get_barrier_semaphore()

    def greet_frame(j, c):
        pl.semaphore_signal(
            barrier, inc=1, device_id=(o, lax.rem(f + j, n_f)), device_id_type=MESH
        )
        return c

    def greet_orient(j, c):
        pl.semaphore_signal(
            barrier, inc=1, device_id=(lax.rem(o + j, n_o), f), device_id_type=MESH
        )
        return c

    lax.fori_loop(1, n_f, greet_frame, 0)
    lax.fori_loop(1, n_o, greet_orient, 0)
    step = frames // LOAD
    for i in range(LOAD):
        pltpu.make_async_copy(
            counts_ref.at[pl.ds(i * step, step)], raw.at[pl.ds(i * step, step)], load_sem.at[i]
        ).start()
    pl.semaphore_wait(barrier, n_f + n_o - 2)

    def to_frame(which, src, dst, peer):
        return pltpu.make_async_remote_copy(
            src_ref=src,
            dst_ref=dst,
            send_sem=frame_send.at[which, peer],
            recv_sem=frame_recv.at[which, f],
            device_id=(o, peer),
            device_id_type=MESH,
        )

    def to_orient(which, src, dst, peer):
        return pltpu.make_async_remote_copy(
            src_ref=src,
            dst_ref=dst,
            send_sem=orient_send.at[which, peer],
            recv_sem=orient_recv.at[which, o],
            device_id=(peer, f),
            device_id_type=MESH,
        )

    def send_frame(which, src, dst):
        def body(j, c):
            peer = lax.rem(f + j, n_f)
            to_frame(which, src(peer), dst, peer).start()
            return c

        lax.fori_loop(1, n_f, body, 0)

    def send_orient(which, src, dst):
        def body(j, c):
            peer = lax.rem(o + j, n_o)
            to_orient(which, src(peer), dst, peer).start()
            return c

        lax.fori_loop(1, n_o, body, 0)

    def from_frame(which, dst, peer):
        pltpu.make_async_remote_copy(
            src_ref=dst,
            dst_ref=dst,
            send_sem=frame_send.at[which, peer],
            recv_sem=frame_recv.at[which, peer],
            device_id=(o, peer),
            device_id_type=MESH,
        ).wait_recv()

    def from_orient(which, dst, peer):
        pltpu.make_async_remote_copy(
            src_ref=dst,
            dst_ref=dst,
            send_sem=orient_send.at[which, peer],
            recv_sem=orient_recv.at[which, peer],
            device_id=(peer, f),
            device_id_type=MESH,
        ).wait_recv()

    def wait_frame(which, dst):
        def body(j, c):
            peer = lax.rem(f + n_f - j, n_f)
            from_frame(which, dst(peer), peer)
            return c

        lax.fori_loop(1, n_f, body, 0)

    def wait_orient(which, dst):
        def body(j, c):
            peer = lax.rem(o + n_o - j, n_o)
            from_orient(which, dst(peer), peer)
            return c

        lax.fori_loop(1, n_o, body, 0)

    def sent_frame(which, src):
        def body(j, c):
            peer = lax.rem(f + j, n_f)
            to_frame(which, src(peer), src(peer), peer).wait_send()
            return c

        lax.fori_loop(1, n_f, body, 0)

    def sent_orient(which, src):
        def body(j, c):
            peer = lax.rem(o + j, n_o)
            to_orient(which, src(peer), src(peer), peer).wait_send()
            return c

        lax.fori_loop(1, n_o, body, 0)

    send_frame(0, lambda peer: codes_ref, codes.at[f])
    send_frame(1, lambda peer: slices_ref, held.at[0, f])
    codes[f] = codes_ref[...]
    held[0, f] = slices_ref[...]

    for i in range(LOAD):
        pltpu.make_async_copy(
            counts_ref.at[pl.ds(i * step, step)], raw.at[pl.ds(i * step, step)], load_sem.at[i]
        ).wait()

        def convert(j, c):
            at = pl.ds(pl.multiple_of(i * step + j * 16, 16), 16)
            high, low = split2(raw[at, :])
            count_high[at, :] = high
            count_low[at, :] = low
            return c

        lax.fori_loop(0, step // 16, convert, 0)

    wait_frame(0, lambda peer: codes.at[peer])
    lane = iota((rows, TILE), 1)
    eye = iota((pair, pair), 0) == iota((pair, pair), 1)
    places = n_o * block

    def prepare(t, c):
        row = codes[t, 0:1, :]
        at = pl.ds(pl.multiple_of(t * pair, pair), pair)

        def fill(i, c):
            here = pl.ds(pl.multiple_of(i * block, block), block)
            place = (iota((block, pair), 0) + i * block).astype(F32)
            gather_to[here, at] = jnp.where(place == row, 1.0, 0.0).astype(BF16)
            return c

        lax.fori_loop(0, n_o, fill, 0)
        column = jnp.sum(jnp.where(eye, row, 0.0), axis=1, keepdims=True)
        place = iota((pair, places), 1).astype(F32)
        gather_from[at, :] = jnp.where(place == column, 1.0, 0.0).astype(BF16)
        shift = jnp.sum(jnp.where(eye, codes[t, 1:2, :], 0.0), axis=1, keepdims=True)
        shift = jnp.broadcast_to(shift[0:rows], (rows, TILE)).astype(jnp.int32)
        shifts[t] = shift
        mark = jnp.where(lane >= shift, 1.0, 0.0)
        marks[at, :] = jnp.concatenate([mark, 1.0 - mark], axis=0).astype(BF16)
        return c

    lax.fori_loop(0, n_f, prepare, 0)

    def count_hits(i, c):
        here = pl.ds(pl.multiple_of((i * n_f + f) * SUB, SUB), SUB)
        place = (iota((SUB, pair), 0) + (i * n_f + f) * SUB).astype(F32)

        def add(t, total):
            at = pl.ds(pl.multiple_of(t * pair, pair), pair)
            chosen = jnp.where(place == codes[t, 0:1, :], 1.0, 0.0).astype(BF16)
            return total + jnp.dot(chosen, marks[at, :], preferred_element_type=F32)

        hits_out[i] = lax.fori_loop(0, n_f, add, jnp.zeros((SUB, TILE), F32))
        return c

    lax.fori_loop(0, n_o, count_hits, 0)
    send_orient(0, lambda peer: hits_out.at[peer], hits_in.at[o])
    hits_in[o] = hits_out[o]

    wait_frame(1, lambda peer: held.at[0, peer])

    def expand(t):
        at = pl.ds(pl.multiple_of(t * pair, pair), pair)
        found = jnp.dot(gather_from[at, :], spread[...], preferred_element_type=F32)
        found = found[:, :TILE] + found[:, TILE:]
        shift = shifts[t]
        value = jnp.where(lane >= shift, found[:rows], found[rows:])
        for k in range(7):
            value = jnp.where(
                (shift & (1 << k)) != 0, pltpu.roll(value, TILE - (1 << k), 1), value
            )
        return value

    def iteration(turn, c):
        def take_logs(t, total):
            value = held[turn, t]
            at = pl.ds(pl.multiple_of(t * TILE, TILE), TILE)
            high, mid, low = split3(jnp.log(value + BACKGROUND))
            logs[0:rows, at] = high
            logs[rows : 2 * rows, at] = mid
            logs[2 * rows : 3 * rows, at] = low
            return total + value

        total = lax.fori_loop(0, n_f, take_logs, jnp.zeros((rows, TILE), F32))
        total = jnp.sum(total, axis=1, keepdims=True)
        across = (((1,), (1,)), ((), ()))
        like = lax.dot_general(
            logs[...], count_high[...], across, preferred_element_type=F32
        ) + lax.dot_general(logs[...], count_low[...], across, preferred_element_type=F32)
        like = like[:rows] + like[rows : 2 * rows] + like[2 * rows :]
        score = SHARPNESS * (like - total * fluence_ref[...])
        top = jnp.max(score, axis=0, keepdims=True)
        expo = jnp.exp(score - top)
        norm = jnp.sum(expo, axis=0, keepdims=True)
        own = stats.at[turn, o]
        for k in range(chunks):
            own[k : k + 1, :] = top[:, k * TILE : (k + 1) * TILE]
            own[chunks + k : chunks + k + 1, :] = norm[:, k * TILE : (k + 1) * TILE]
        send_orient(1 + turn, lambda peer: stats.at[turn, o], stats.at[turn, o])
        wait_orient(1 + turn, lambda peer: stats.at[turn, peer])
        peak = stats[turn, 0, 0:chunks, :]
        for i in range(1, n_o):
            peak = jnp.maximum(peak, stats[turn, i, 0:chunks, :])
        whole = jnp.zeros((chunks, TILE), F32)
        for i in range(n_o):
            whole = whole + stats[turn, i, chunks : 2 * chunks, :] * jnp.exp(
                stats[turn, i, 0:chunks, :] - peak
            )
        factor = jnp.exp(stats[turn, o, 0:chunks, :] - peak) / whole
        factor = jnp.concatenate([factor[k : k + 1, :] for k in range(chunks)], axis=1)
        prob = expo * factor
        den = jnp.sum(prob * fluence_ref[...], axis=1, keepdims=True)
        den = jnp.sum(
            jnp.where(iota((rows, TILE), 0) == lane, den, 0.0), axis=0, keepdims=True
        )
        dens[turn, f] = jnp.broadcast_to(den, (SUB, TILE))
        send_frame(2 + turn, lambda peer: dens.at[turn, f], dens.at[turn, f])
        probs = jnp.concatenate(split2(prob), axis=0)
        num = jnp.dot(probs, count_high[...], preferred_element_type=F32) + jnp.dot(
            probs, count_low[...], preferred_element_type=F32
        )
        num = num[:rows] + num[rows:]
        wait_frame(2 + turn, lambda peer: dens.at[turn, peer])
        weight = dens[turn, 0]
        for i in range(1, n_f):
            weight = weight + dens[turn, i]
        weight = jnp.sum(
            jnp.where(iota((rows, TILE), 0) == lane, weight[0:1, :], 0.0),
            axis=1,
            keepdims=True,
        )
        inverse = 1.0 / (weight + 1.0)

        for t in range(n_f):
            value = num[:, t * TILE : (t + 1) * TILE]
            value = (value + jnp.where(f == t, held[turn, t], 0.0)) * inverse
            shift = shifts[t]
            for k in range(7):
                value = jnp.where((shift & (1 << k)) != 0, pltpu.roll(value, 1 << k, 1), value)
            high, low = split2(value)
            first = lane >= shift
            none = jnp.zeros((rows, TILE), BF16)
            at = t * pair
            tiles[at : at + rows, :TILE] = jnp.where(first, high, none)
            tiles[at : at + rows, TILE:] = jnp.where(first, low, none)
            tiles[at + rows : at + pair, :TILE] = jnp.where(first, none, high)
            tiles[at + rows : at + pair, TILE:] = jnp.where(first, none, low)

        def collect(i):
            here = pl.ds(pl.multiple_of(i * block, block), block)
            part = jnp.dot(gather_to[here, :], tiles[...], preferred_element_type=F32)
            return part[:, :TILE] + part[:, TILE:]

        def scatter(j, c):
            peer = lax.rem(o + j, n_o)
            part_out[turn, peer] = collect(peer)
            to_orient(3 + turn, part_out.at[turn, peer], part_in.at[turn, o], peer).start()
            return c

        lax.fori_loop(1, n_o, scatter, 0)
        part_in[turn, o] = collect(o)
        wait_orient(3 + turn, lambda peer: part_in.at[turn, peer])
        part = part_in[turn, 0]
        for i in range(1, n_o):
            part = part + part_in[turn, i]
        for i in range(n_f):
            brick_out[turn, i] = part[i * SUB : (i + 1) * SUB]
        send_frame(4 + turn, lambda peer: brick_out.at[turn, peer], brick_in.at[turn, f])
        brick_in[turn, f] = brick_out[turn, f]

        @pl.when(turn == 0)
        def _():
            wait_orient(0, lambda peer: hits_in.at[peer])

        hits = hits_in[0]
        for i in range(1, n_o):
            hits = hits + hits_in[i]
        wait_frame(4 + turn, lambda peer: brick_in.at[turn, peer])
        brick = brick_in[turn, 0]
        for i in range(1, n_f):
            brick = brick + brick_in[turn, i]
        brick = brick / jnp.maximum(hits, 1.0)
        out_ref[...] = brick
        volume[turn, o, f] = brick
        send_frame(6 + turn, lambda peer: volume.at[turn, o, f], volume.at[turn, o, f])
        wait_frame(6 + turn, lambda peer: volume.at[turn, o, peer])
        send_orient(5 + turn, lambda peer: volume.at[turn, o], volume.at[turn, o])
        wait_orient(5 + turn, lambda peer: volume.at[turn, peer])
        for i in range(n_o):
            high, low = split2(volume[turn, i].reshape(block, TILE))
            spread[i * block : (i + 1) * block, :TILE] = high
            spread[i * block : (i + 1) * block, TILE:] = low

        @pl.when(turn < ITERS - 1)
        def _():
            def fill(t, c):
                held[turn + 1, t] = expand(t)
                return c

            lax.fori_loop(0, n_f, fill, 0)

        return c

    lax.fori_loop(0, ITERS, iteration, 0)
    new_ref[...] = expand(f)

    sent_frame(0, lambda peer: codes_ref)
    sent_frame(1, lambda peer: slices_ref)
    sent_orient(0, lambda peer: hits_out.at[peer])

    def finish(turn, c):
        sent_frame(2 + turn, lambda peer: dens.at[turn, f])
        sent_frame(4 + turn, lambda peer: brick_out.at[turn, peer])
        sent_frame(6 + turn, lambda peer: volume.at[turn, o, f])
        sent_orient(1 + turn, lambda peer: stats.at[turn, o])
        sent_orient(3 + turn, lambda peer: part_out.at[turn, peer])
        sent_orient(5 + turn, lambda peer: volume.at[turn, o])
        return c

    lax.fori_loop(0, ITERS, finish, 0)


def on_device(n_o, n_f, slices, counts, fluence, tile_brick, tile_base):
    rows = slices.shape[0]
    frames, pixels = counts.shape
    pair = 2 * rows
    block = n_f * SUB
    places = n_o * block
    code = tile_brick[:, :, 0] * VOX + tile_base
    place = code // TILE
    shift = code % TILE
    codes = jnp.concatenate(
        [
            jnp.concatenate([place, place + 1], axis=1),
            jnp.concatenate([shift, shift], axis=1),
            jnp.zeros((SUB - 2, pair), jnp.int32),
        ],
        axis=0,
    ).astype(F32)
    vmem = pl.BlockSpec(memory_space=pltpu.VMEM)
    new, brick = pl.pallas_call(
        functools.partial(kernel, n_o, n_f),
        out_shape=(
            jax.ShapeDtypeStruct((rows, TILE), F32),
            jax.ShapeDtypeStruct((SUB, TILE), F32),
        ),
        in_specs=[vmem, vmem, vmem, pl.BlockSpec(memory_space=pl.ANY)],
        out_specs=(vmem, vmem),
        scratch_shapes=[
            pltpu.VMEM((frames, pixels), F32),
            pltpu.VMEM((frames, pixels), BF16),
            pltpu.VMEM((frames, pixels), BF16),
            pltpu.VMEM((ITERS, n_f, rows, TILE), F32),
            pltpu.VMEM((n_f, SUB, pair), F32),
            pltpu.VMEM((ITERS, n_o, 2 * (frames // TILE), TILE), F32),
            pltpu.VMEM((ITERS, n_f, SUB, TILE), F32),
            pltpu.VMEM((places, n_f * pair), BF16),
            pltpu.VMEM((n_f * pair, places), BF16),
            pltpu.VMEM((n_f, rows, TILE), jnp.int32),
            pltpu.VMEM((n_f * pair, 2 * TILE), BF16),
            pltpu.VMEM((n_f * pair, TILE), BF16),
            pltpu.VMEM((3 * rows, pixels), BF16),
            pltpu.VMEM((ITERS, n_o, block, TILE), F32),
            pltpu.VMEM((ITERS, n_o, block, TILE), F32),
            pltpu.VMEM((ITERS, n_f, SUB, TILE), F32),
            pltpu.VMEM((ITERS, n_f, SUB, TILE), F32),
            pltpu.VMEM((ITERS, n_o, n_f, SUB, TILE), F32),
            pltpu.VMEM((places, 2 * TILE), BF16),
            pltpu.VMEM((n_o, SUB, TILE), F32),
            pltpu.VMEM((n_o, SUB, TILE), F32),
            pltpu.SemaphoreType.DMA((LOAD,)),
            pltpu.SemaphoreType.DMA((2 + 3 * ITERS, n_f)),
            pltpu.SemaphoreType.DMA((2 + 3 * ITERS, n_f)),
            pltpu.SemaphoreType.DMA((1 + 3 * ITERS, n_o)),
            pltpu.SemaphoreType.DMA((1 + 3 * ITERS, n_o)),
        ],
        compiler_params=pltpu.CompilerParams(
            collective_id=0, has_side_effects=True, vmem_limit_bytes=60 << 20
        ),
    )(slices, codes, fluence[None, :], counts)
    return new, brick.reshape(1, SUB * TILE)


def solution(mesh):
    n_o, n_f = mesh.shape["orient"], mesh.shape["frame"]
    in_specs = (
        P("orient", "frame"),
        P("frame", None),
        P("frame"),
        P("frame", "orient", None),
        P("frame", "orient"),
    )
    out_specs = (P("orient", "frame"), P(("orient", "frame"), None))
    return jax.shard_map(
        functools.partial(on_device, n_o, n_f),
        mesh=mesh,
        in_specs=in_specs,
        out_specs=out_specs,
        check_vma=False,
    )
```

time: 359 us -> 141 us (0.39)
  blocking collectives: 230 us -> 0 us
  Pallas kernels: 0 us -> 136 us
  waiting for transfers between devices: 50.9 us -> 0 us
  matrix products: 32.6 us -> 0 us
  starting transfers between devices: 20.4 us -> 0 us
  between operations: 14.4 us -> 0.65 us
  local copies, waits for them, and re-layouts: 8.55 us -> 2.72 us
    pallas_call x0 -> x1, Pallas kernels: none -> 136 us  [on_device(): pl.pallas_call(functools.partial(kernel, n_o, n_f), out_shape=(jax.ShapeD...]
    psum x4 -> x0, blocking collectives: 99.6 us -> none  [the longest x2 73.8 us: on_device(): weight = lax.psum(jnp.dot(prob, fluence, precision=highest), 'frame')]
    all_to_all x3 -> x0, blocking collectives: 50 us -> none  [the longest x2 29.9 us: on_device(): lax.all_to_all(looked, ('orient', 'frame'), split_axis=0, concat_axis=0,...]
    all_gather x2 -> x0, blocking collectives: 49.9 us -> none  [on_device(): piece = lax.all_gather(local, 'frame', axis=1, tiled=True)]
    reduce_scatter x2 -> x0, waiting for transfers between devices: 42.5 us -> none  [on_device(): lax.psum_scatter(lax.dot_general(counts, prob, (((0,), (1,)), ((), ())),...]
    dot_general x12 -> x0, matrix products: 30.3 us -> none  [the longest x2 12.6 us: on_device(): lax.dot_general(jnp.log(piece + BACKGROUND), counts, (((1,), (1,)), ((),...]
    pmax x2 -> x0, blocking collectives: 30.1 us -> none  [on_device(): peak = lax.pmax(top, 'orient')]
    all_to_all x2 -> x0, starting transfers between devices: 20.2 us -> none  [the longest x1 10.8 us: on_device(): lax.all_to_all(bases, ('orient', 'frame'), split_axis=0, concat_axis=0, t...]
  transfers between devices with their start and end apart: 4 -> 0, of which waited for: 3 -> 0; matrix products, arithmetic and copies ran while one was open for 3% -> 0% of each run, Pallas kernels for 0% -> 0%
where the time goes in v1:
time: 141 us
  Pallas kernels  136 us (96%)
  local copies, waits for them, and re-layouts  2.72 us (2%)
    pallas_call x1, Pallas kernels, on_device(): pl.pallas_call(functools.partial(kernel, n_o, n_f), out_shape=(jax.ShapeD...  136 us

profile of v1, /device:TPU:1, one launch (start us, length us, event | category | flops | bytes accessed | tf_op | source)
XLA Modules:
  0.0 140.8 jit_solution(6727771720746632712)
XLA Ops:
  0.6 0.1 pad.4.clone
  0.7 0.7 broadcast_add_fusion
  1.4 0.7 add_convert_fusion.codes_ref
  2.1 136.0 %shard_map.68 = (f32[64,128]{1,0:T(8,128)}, f32[8,128]{1,0:T(8,128)}) custom-call(f32[64,128]{1,0:T(8,128)} %slices_ref.1, f32[8,128]{1,0:T(8,128)} %add_convert_fusion.codes_ref, f32[1,512]{1,0:T(1,128)} %bitcast.11, f32[512,2048]{1,0:T(8,128)} %counts_ref.1), custom_call_target="tpu_custom_call" | custom-call | tf_op jit(solution)/shard_map/pallas_call | solution.py:437
  138.1 1.4 copy.9
  139.5 1.3 copy.10
  (2 shorter events, 0.0 us)

commit v2 on v1

v2 whole, which is shorter than its diff:
```python
import functools

import jax
import jax.numpy as jnp
from jax import lax
from jax.experimental import pallas as pl
from jax.experimental.pallas import tpu as pltpu
from jax.sharding import PartitionSpec as P

VOX = 1024
TILE = 128
SUB = VOX // TILE
ITERS = 2
BACKGROUND = 0.1
SHARPNESS = 0.02
MESH = pl.DeviceIdType.MESH
F32 = jnp.float32
BF16 = jnp.bfloat16
LOAD = 4


def split2(x):
    high = x.astype(BF16)
    return high, (x - high.astype(F32)).astype(BF16)


def split3(x):
    high = x.astype(BF16)
    rest = x - high.astype(F32)
    mid = rest.astype(BF16)
    return high, mid, (rest - mid.astype(F32)).astype(BF16)


def iota(shape, axis):
    return lax.broadcasted_iota(jnp.int32, shape, axis)


def kernel(
    n_o,
    n_f,
    slices_ref,
    codes_ref,
    fluence_ref,
    counts_ref,
    new_ref,
    out_ref,
    raw,
    count_high,
    count_low,
    held,
    codes,
    stats,
    dens,
    gather_to,
    gather_from,
    shifts,
    moved,
    tiles,
    marks,
    logs,
    part_out,
    part_in,
    volume,
    spread,
    hits_out,
    hits_in,
    load_sem,
    send_sem,
    recv_sem,
):
    o = lax.axis_index("orient")
    f = lax.axis_index("frame")
    n = n_o * n_f
    me = o * n_f + f
    rows = slices_ref.shape[0]
    frames = counts_ref.shape[0]
    pair = 2 * rows
    block = n_f * SUB
    places = n_o * block
    chunks = frames // TILE

    barrier = pltpu.get_barrier_semaphore()

    def greet(j, c):
        peer = lax.rem(me + j, n)
        pl.semaphore_signal(
            barrier,
            inc=1,
            device_id=(lax.div(peer, n_f), lax.rem(peer, n_f)),
            device_id_type=MESH,
        )
        return c

    lax.fori_loop(1, n, greet, 0)
    step = frames // LOAD
    for i in range(LOAD):
        pltpu.make_async_copy(
            counts_ref.at[pl.ds(i * step, step)], raw.at[pl.ds(i * step, step)], load_sem.at[i]
        ).start()
    pl.semaphore_wait(barrier, n - 1)

    def copy(which, src, dst, to):
        return pltpu.make_async_remote_copy(
            src_ref=src,
            dst_ref=dst,
            send_sem=send_sem.at[which],
            recv_sem=recv_sem.at[which],
            device_id=to,
            device_id_type=MESH,
        )

    def send_frame(which, src, dst):
        def body(j, c):
            peer = lax.rem(f + j, n_f)
            copy(which, src(peer), dst, (o, peer)).start()
            return c

        lax.fori_loop(1, n_f, body, 0)

    def send_orient(which, src, dst):
        def body(j, c):
            peer = lax.rem(o + j, n_o)
            copy(which, src(peer), dst, (peer, f)).start()
            return c

        lax.fori_loop(1, n_o, body, 0)

    def received(which, whole):
        copy(which, whole, whole, (lax.rem(o + 1, n_o), f)).wait_recv()

    def sent(which, whole):
        copy(which, whole, whole, (lax.rem(o + 1, n_o), f)).wait_send()

    send_frame(0, lambda peer: codes_ref, codes.at[f])
    send_frame(1, lambda peer: slices_ref, held.at[0, f])
    codes[f] = codes_ref[...]
    held[0, f] = slices_ref[...]

    for i in range(LOAD):
        pltpu.make_async_copy(
            counts_ref.at[pl.ds(i * step, step)], raw.at[pl.ds(i * step, step)], load_sem.at[i]
        ).wait()

        def convert(j, c):
            at = pl.ds(pl.multiple_of(i * step + j * 16, 16), 16)
            high, low = split2(raw[at, :])
            count_high[at, :] = high
            count_low[at, :] = low
            return c

        lax.fori_loop(0, step // 16, convert, 0)

    received(0, codes.at[pl.ds(0, n_f - 1)])
    lane = iota((rows, TILE), 1)
    diagonal = iota((rows, TILE), 0) == lane
    eye = iota((pair, pair), 0) == iota((pair, pair), 1)

    def prepare(t, c):
        row = codes[t, 0:1, :]
        at = pl.ds(pl.multiple_of(t * pair, pair), pair)

        def fill(i, c):
            here = pl.ds(pl.multiple_of(i * block, block), block)
            place = (iota((block, pair), 0) + i * block).astype(F32)
            gather_to[here, at] = jnp.where(place == row, 1.0, 0.0).astype(BF16)
            return c

        lax.fori_loop(0, n_o, fill, 0)
        column = jnp.sum(jnp.where(eye, row, 0.0), axis=1, keepdims=True)
        place = iota((pair, places), 1).astype(F32)
        gather_from[at, :] = jnp.where(place == column, 1.0, 0.0).astype(BF16)
        shift = jnp.sum(jnp.where(eye, codes[t, 1:2, :], 0.0), axis=1, keepdims=True)
        shift = jnp.broadcast_to(shift[0:rows], (rows, TILE)).astype(jnp.int32)
        shifts[t] = shift
        mark = jnp.where(lane >= shift, 1.0, 0.0)
        marks[at, :] = jnp.concatenate([mark, 1.0 - mark], axis=0).astype(BF16)
        return c

    lax.fori_loop(0, n_f, prepare, 0)
    received(1, held.at[0, pl.ds(0, n_f - 1)])

    def count_hits():
        index = iota((n_o * SUB, pair), 0)
        place = (lax.div(index, SUB) * block + f * SUB + lax.rem(index, SUB)).astype(F32)
        chosen = jnp.concatenate(
            [jnp.where(place == codes[t, 0:1, :], 1.0, 0.0).astype(BF16) for t in range(n_f)],
            axis=1,
        )
        hits = jnp.dot(chosen, marks[...], preferred_element_type=F32)
        for i in range(n_o):
            hits_out[i] = hits[i * SUB : (i + 1) * SUB]
        send_orient(2, lambda peer: hits_out.at[peer], hits_in.at[o])
        hits_in[o] = hits_out[o]

    def expand(t):
        at = pl.ds(pl.multiple_of(t * pair, pair), pair)
        found = jnp.dot(gather_from[at, :], spread[...], preferred_element_type=F32)
        found = found[:, :TILE] + found[:, TILE:]
        shift = shifts[t]
        value = jnp.where(lane >= shift, found[:rows], found[rows:])
        for k in range(7):
            value = jnp.where(
                (shift & (1 << k)) != 0, pltpu.roll(value, TILE - (1 << k), 1), value
            )
        return value

    def iteration(turn, c):
        def take_logs(t, total):
            value = held[turn, t]
            at = pl.ds(pl.multiple_of(t * TILE, TILE), TILE)
            high, mid, low = split3(jnp.log(value + BACKGROUND))
            logs[0:rows, at] = high
            logs[rows : 2 * rows, at] = mid
            logs[2 * rows : 3 * rows, at] = low
            return total + value

        total = lax.fori_loop(0, n_f, take_logs, jnp.zeros((rows, TILE), F32))
        total = jnp.sum(total, axis=1, keepdims=True)
        across = (((1,), (1,)), ((), ()))
        like = lax.dot_general(
            logs[...], count_high[...], across, preferred_element_type=F32
        ) + lax.dot_general(logs[...], count_low[...], across, preferred_element_type=F32)
        like = like[:rows] + like[rows : 2 * rows] + like[2 * rows :]
        score = SHARPNESS * (like - total * fluence_ref[...])
        top = jnp.max(score, axis=0, keepdims=True)
        expo = jnp.exp(score - top)
        norm = jnp.sum(expo, axis=0, keepdims=True)
        own = stats.at[turn, o]
        for k in range(chunks):
            own[k : k + 1, :] = top[:, k * TILE : (k + 1) * TILE]
            own[chunks + k : chunks + k + 1, :] = norm[:, k * TILE : (k + 1) * TILE]
        send_orient(3 + turn, lambda peer: stats.at[turn, o], stats.at[turn, o])

        @pl.when(turn == 0)
        def _():
            count_hits()

        received(3 + turn, stats.at[turn, pl.ds(0, n_o - 1)])
        peak = stats[turn, 0, 0:chunks, :]
        for i in range(1, n_o):
            peak = jnp.maximum(peak, stats[turn, i, 0:chunks, :])
        whole = jnp.zeros((chunks, TILE), F32)
        for i in range(n_o):
            whole = whole + stats[turn, i, chunks : 2 * chunks, :] * jnp.exp(
                stats[turn, i, 0:chunks, :] - peak
            )
        factor = jnp.exp(stats[turn, o, 0:chunks, :] - peak) / whole
        factor = jnp.concatenate([factor[k : k + 1, :] for k in range(chunks)], axis=1)
        prob = expo * factor
        den = jnp.sum(prob * fluence_ref[...], axis=1, keepdims=True)
        dens[turn, f] = jnp.sum(jnp.where(diagonal, den, 0.0), axis=0, keepdims=True)
        send_frame(5 + turn, lambda peer: dens.at[turn, f], dens.at[turn, f])

        probs = jnp.concatenate(split2(prob), axis=0)
        num = jnp.dot(probs, count_high[...], preferred_element_type=F32) + jnp.dot(
            probs, count_low[...], preferred_element_type=F32
        )
        num = num[:rows] + num[rows:]
        for t in range(n_f):
            value = num[:, t * TILE : (t + 1) * TILE] + jnp.where(f == t, held[turn, t], 0.0)
            shift = shifts[t]
            for k in range(7):
                value = jnp.where((shift & (1 << k)) != 0, pltpu.roll(value, 1 << k, 1), value)
            moved[t] = value
        received(5 + turn, dens.at[turn, pl.ds(0, n_f - 1)])
        weight = dens[turn, 0]
        for i in range(1, n_f):
            weight = weight + dens[turn, i]
        weight = jnp.sum(jnp.where(diagonal, weight, 0.0), axis=1, keepdims=True)
        inverse = 1.0 / (weight + 1.0)
        for t in range(n_f):
            high, low = split2(moved[t] * inverse)
            first = lane >= shifts[t]
            none = jnp.zeros((rows, TILE), BF16)
            at = t * pair
            tiles[at : at + rows, :TILE] = jnp.where(first, high, none)
            tiles[at : at + rows, TILE:] = jnp.where(first, low, none)
            tiles[at + rows : at + pair, :TILE] = jnp.where(first, none, high)
            tiles[at + rows : at + pair, TILE:] = jnp.where(first, none, low)

        def collect(i):
            here = pl.ds(pl.multiple_of(i * block, block), block)
            part = jnp.dot(gather_to[here, :], tiles[...], preferred_element_type=F32)
            part = part[:, :TILE] + part[:, TILE:]
            for k in range(n_f):
                part_out[turn, i * n_f + k] = part[k * SUB : (k + 1) * SUB]

        def give(peer_o, peer_f):
            copy(
                7 + turn,
                part_out.at[turn, peer_o * n_f + peer_f],
                part_in.at[turn, me],
                (peer_o, peer_f),
            ).start()

        def scatter(j, c):
            peer = lax.rem(o + j, n_o)
            collect(peer)

            def each(k, c):
                give(peer, lax.rem(f + k, n_f))
                return c

            lax.fori_loop(0, n_f, each, 0)
            return c

        lax.fori_loop(1, n_o, scatter, 0)
        collect(o)

        def each(k, c):
            give(o, lax.rem(f + k, n_f))
            return c

        lax.fori_loop(1, n_f, each, 0)
        part_in[turn, me] = part_out[turn, me]

        @pl.when(turn == 0)
        def _():
            received(2, hits_in.at[pl.ds(0, n_o - 1)])

        hits = jnp.sum(hits_in[...], axis=0)
        received(7 + turn, part_in.at[turn, pl.ds(0, n - 1)])
        brick = jnp.sum(part_in[turn], axis=0) / jnp.maximum(hits, 1.0)
        out_ref[...] = brick
        volume[turn, me] = brick

        def spread_out(j, c):
            peer = lax.rem(me + j, n)
            copy(
                9 + turn,
                volume.at[turn, me],
                volume.at[turn, me],
                (lax.div(peer, n_f), lax.rem(peer, n_f)),
            ).start()
            return c

        lax.fori_loop(1, n, spread_out, 0)
        received(9 + turn, volume.at[turn, pl.ds(0, n - 1)])
        high, low = split2(volume[turn].reshape(places, TILE))
        spread[:, :TILE] = high
        spread[:, TILE:] = low

        @pl.when(turn < ITERS - 1)
        def _():
            def fill(t, c):
                for k in range(4):
                    held[turn + 1, t * 4 + k] = expand(t * 4 + k)
                return c

            lax.fori_loop(0, n_f // 4, fill, 0)

        return c

    lax.fori_loop(0, ITERS, iteration, 0)
    new_ref[...] = expand(f)

    sent(0, codes.at[pl.ds(0, n_f - 1)])
    sent(1, held.at[0, pl.ds(0, n_f - 1)])
    sent(2, hits_out.at[pl.ds(0, n_o - 1)])
    for turn in range(ITERS):
        sent(3 + turn, stats.at[turn, pl.ds(0, n_o - 1)])
        sent(5 + turn, dens.at[turn, pl.ds(0, n_f - 1)])
        sent(7 + turn, part_out.at[turn, pl.ds(0, n - 1)])
        sent(9 + turn, volume.at[turn, pl.ds(0, n - 1)])


def on_device(n_o, n_f, slices, counts, fluence, tile_brick, tile_base):
    rows = slices.shape[0]
    frames, pixels = counts.shape
    pair = 2 * rows
    block = n_f * SUB
    places = n_o * block
    code = tile_brick[:, :, 0] * VOX + tile_base
    place = code // TILE
    shift = code % TILE
    codes = jnp.concatenate(
        [
            jnp.concatenate([place, place + 1], axis=1),
            jnp.concatenate([shift, shift], axis=1),
            jnp.zeros((SUB - 2, pair), jnp.int32),
        ],
        axis=0,
    ).astype(F32)
    vmem = pl.BlockSpec(memory_space=pltpu.VMEM)
    new, brick = pl.pallas_call(
        functools.partial(kernel, n_o, n_f),
        out_shape=(
            jax.ShapeDtypeStruct((rows, TILE), F32),
            jax.ShapeDtypeStruct((SUB, TILE), F32),
        ),
        in_specs=[vmem, vmem, vmem, pl.BlockSpec(memory_space=pl.ANY)],
        out_specs=(vmem, vmem),
        scratch_shapes=[
            pltpu.VMEM((frames, pixels), F32),
            pltpu.VMEM((frames, pixels), BF16),
            pltpu.VMEM((frames, pixels), BF16),
            pltpu.VMEM((ITERS, n_f, rows, TILE), F32),
            pltpu.VMEM((n_f, SUB, pair), F32),
            pltpu.VMEM((ITERS, n_o, 2 * (frames // TILE), TILE), F32),
            pltpu.VMEM((ITERS, n_f, 1, TILE), F32),
            pltpu.VMEM((places, n_f * pair), BF16),
            pltpu.VMEM((n_f * pair, places), BF16),
            pltpu.VMEM((n_f, rows, TILE), jnp.int32),
            pltpu.VMEM((n_f, rows, TILE), F32),
            pltpu.VMEM((n_f * pair, 2 * TILE), BF16),
            pltpu.VMEM((n_f * pair, TILE), BF16),
            pltpu.VMEM((3 * rows, pixels), BF16),
            pltpu.VMEM((ITERS, n_o * n_f, SUB, TILE), F32),
            pltpu.VMEM((ITERS, n_o * n_f, SUB, TILE), F32),
            pltpu.VMEM((ITERS, n_o * n_f, SUB, TILE), F32),
            pltpu.VMEM((places, 2 * TILE), BF16),
            pltpu.VMEM((n_o, SUB, TILE), F32),
            pltpu.VMEM((n_o, SUB, TILE), F32),
            pltpu.SemaphoreType.DMA((LOAD,)),
            pltpu.SemaphoreType.DMA((3 + 4 * ITERS,)),
            pltpu.SemaphoreType.DMA((3 + 4 * ITERS,)),
        ],
        compiler_params=pltpu.CompilerParams(
            collective_id=0, has_side_effects=True, vmem_limit_bytes=60 << 20
        ),
    )(slices, codes, fluence[None, :], counts)
    return new, brick.reshape(1, SUB * TILE)


def solution(mesh):
    n_o, n_f = mesh.shape["orient"], mesh.shape["frame"]
    in_specs = (
        P("orient", "frame"),
        P("frame", None),
        P("frame"),
        P("frame", "orient", None),
        P("frame", "orient"),
    )
    out_specs = (P("orient", "frame"), P(("orient", "frame"), None))
    return jax.shard_map(
        functools.partial(on_device, n_o, n_f),
        mesh=mesh,
        in_specs=in_specs,
        out_specs=out_specs,
        check_vma=False,
    )
```

time: 141 us -> 94.7 us (0.67)
  Pallas kernels: 136 us -> 89.7 us
    pallas_call x1, Pallas kernels: 136 us -> 89.7 us  [on_device(): pl.pallas_call(functools.partial(kernel, n_o, n_f), out_shape=(jax.ShapeD...]
where the time goes in v2:
time: 94.7 us; the launch traced here: 94.4 us
  Pallas kernels  89.7 us (95%)
  local copies, waits for them, and re-layouts  2.72 us (3%)
  other arithmetic  1.36 us (1%)
    pallas_call x1, Pallas kernels, on_device(): pl.pallas_call(functools.partial(kernel, n_o, n_f), out_shape=(jax.ShapeD...  89.7 us
    unnamed x2, local copies, waits for them, and re-layouts  2.64 us

profile of v2, /device:TPU:1, one launch (start us, length us, event | category | flops | bytes accessed | tf_op | source)
XLA Modules:
  0.0 94.4 jit_solution(15258392962928822165)
XLA Ops:
  0.6 0.1 pad.4.clone
  0.7 0.7 broadcast_add_fusion
  1.4 0.7 add_convert_fusion.codes_ref
  2.1 89.7 %shard_map.68 = (f32[64,128]{1,0:T(8,128)}, f32[8,128]{1,0:T(8,128)}) custom-call(f32[64,128]{1,0:T(8,128)} %slices_ref.1, f32[8,128]{1,0:T(8,128)} %add_convert_fusion.codes_ref, f32[1,512]{1,0:T(1,128)} %bitcast.11, f32[512,2048]{1,0:T(8,128)} %counts_ref.1), custom_call_target="tpu_custom_call" | custom-call | tf_op jit(solution)/shard_map/pallas_call | solution.py:385
  91.8 1.4 %copy.9 = f32[64,128]{1,0:T(8,128)} copy(f32[64,128]{1,0:T(8,128)} %get-tuple-element.11) | data formatting | bytes 65536
  93.2 1.3 %copy.10 = f32[1,1024]{1,0:T(1,128)} copy(f32[1,1024]{1,0:T(1,128)} %bitcast.10) | data formatting | bytes 8192
  (2 shorter events, 0.0 us)

commit v3 on v2

--- a/solution.py
+++ b/solution.py
@@ -39,7 +39,8 @@
     n_o,
     n_f,
     slices_ref,
-    codes_ref,
+    brick_ref,
+    base_ref,
     fluence_ref,
     counts_ref,
     new_ref,
@@ -48,7 +49,6 @@
     count_high,
     count_low,
     held,
-    codes,
     stats,
     dens,
     gather_to,
@@ -67,6 +67,10 @@
     load_sem,
     send_sem,
     recv_sem,
+    first_recv,
+    first_pass,
+    wide_recv,
+    wide_pass,
 ):
     o = lax.axis_index("orient")
     f = lax.axis_index("frame")
@@ -78,6 +82,13 @@
     block = n_f * SUB
     places = n_o * block
     chunks = frames // TILE
+    half = n_f // 2
+    ring = n_f // 4
+    core = lax.rem(f, 2)
+    chip = lax.div(f, 2)
+    sibling = f + 1 - 2 * core
+    mine = core * half + chip
+    lane = iota((rows, TILE), 1)
 
     barrier = pltpu.get_barrier_semaphore()
 
@@ -97,6 +108,34 @@
         pltpu.make_async_copy(
             counts_ref.at[pl.ds(i * step, step)], raw.at[pl.ds(i * step, step)], load_sem.at[i]
         ).start()
+
+    held[0, f, 0:rows] = slices_ref[...]
+    named = brick_ref[...]
+    inside = lax.rem(named, n_f)
+    place = (
+        lax.div(named, n_f) * block
+        + (lax.rem(inside, 2) * half + lax.div(inside, 2)) * SUB
+        + lax.div(base_ref[...], TILE)
+    )
+    shift = lax.rem(base_ref[...], TILE)
+    held[0, f, rows : rows + 1] = jnp.concatenate([place, place + 1], axis=1).astype(F32)
+    held[0, f, rows + 1 : rows + 2] = jnp.concatenate([shift, shift], axis=1).astype(F32)
+    held[0, f, rows + 2 : rows + SUB] = jnp.zeros((SUB - 2, TILE), F32)
+
+    for i in range(LOAD):
+        pltpu.make_async_copy(
+            counts_ref.at[pl.ds(i * step, step)], raw.at[pl.ds(i * step, step)], load_sem.at[i]
+        ).wait()
+
+        def convert(j, c):
+            at = pl.ds(pl.multiple_of(i * step + j * 16, 16), 16)
+            high, low = split2(raw[at, :])
+            count_high[at, :] = high
+            count_low[at, :] = low
+            return c
+
+        lax.fori_loop(0, step // 16, convert, 0)
+
     pl.semaphore_wait(barrier, n - 1)
 
     def copy(which, src, dst, to):
@@ -131,32 +170,67 @@
     def sent(which, whole):
         copy(which, whole, whole, (lax.rem(o + 1, n_o), f)).wait_send()
 
-    send_frame(0, lambda peer: codes_ref, codes.at[f])
-    send_frame(1, lambda peer: slices_ref, held.at[0, f])
-    codes[f] = codes_ref[...]
-    held[0, f] = slices_ref[...]
-
-    for i in range(LOAD):
-        pltpu.make_async_copy(
-            counts_ref.at[pl.ds(i * step, step)], raw.at[pl.ds(i * step, step)], load_sem.at[i]
-        ).wait()
-
-        def convert(j, c):
-            at = pl.ds(pl.multiple_of(i * step + j * 16, 16), 16)
-            high, low = split2(raw[at, :])
-            count_high[at, :] = high
-            count_low[at, :] = low
-            return c
-
-        lax.fori_loop(0, step // 16, convert, 0)
-
-    received(0, codes.at[pl.ds(0, n_f - 1)])
-    lane = iota((rows, TILE), 1)
+    def chip_at(k):
+        x = lax.rem(lax.div(chip, 2) + lax.div(k, 2) + ring // 2, ring)
+        return x * 2 + lax.rem(chip + 1 + k, 2)
+
+    def far_first(i):
+        return lax.rem(o + n_o // 2 + (1 - 2 * lax.rem(i, 2)) * lax.div(i + 1, 2), n_o)
+
+    def deliver(src, dst, out, into, to):
+        return pltpu.make_async_remote_copy(
+            src_ref=src,
+            dst_ref=dst,
+            send_sem=out,
+            recv_sem=into,
+            device_id=to,
+            device_id_type=MESH,
+        )
+
+    def pass_first(at):
+        packet = held.at[0, at * 2 + core]
+        deliver(packet, packet, send_sem.at[1], first_pass.at[at], (o, sibling)).start()
+
+    def send_first(k, c):
+        at = chip_at(k)
+
+        @pl.when(at != chip)
+        def _():
+            packet = held.at[0, f]
+            deliver(
+                packet, packet, send_sem.at[0], first_recv.at[chip], (o, at * 2 + core)
+            ).start()
+
+        return c
+
+    lax.fori_loop(0, half, send_first, 0)
+    pass_first(chip)
+
+    def relay_first(k, c):
+        at = chip_at(half - 1 - k)
+
+        @pl.when(at != chip)
+        def _():
+            packet = held.at[0, at * 2 + core]
+            deliver(packet, packet, send_sem.at[0], first_recv.at[at], (o, sibling)).wait_recv()
+            pass_first(at)
+
+        return c
+
+    lax.fori_loop(0, half, relay_first, 0)
+
+    def land_first(k, c):
+        at = chip_at(half - 1 - k)
+        packet = held.at[0, at * 2 + 1 - core]
+        deliver(packet, packet, send_sem.at[1], first_pass.at[at], (o, sibling)).wait_recv()
+        return c
+
+    lax.fori_loop(0, half, land_first, 0)
     diagonal = iota((rows, TILE), 0) == lane
     eye = iota((pair, pair), 0) == iota((pair, pair), 1)
 
     def prepare(t, c):
-        row = codes[t, 0:1, :]
+        row = held[0, t, rows : rows + 1]
         at = pl.ds(pl.multiple_of(t * pair, pair), pair)
 
         def fill(i, c):
@@ -169,7 +243,7 @@
         column = jnp.sum(jnp.where(eye, row, 0.0), axis=1, keepdims=True)
         place = iota((pair, places), 1).astype(F32)
         gather_from[at, :] = jnp.where(place == column, 1.0, 0.0).astype(BF16)
-        shift = jnp.sum(jnp.where(eye, codes[t, 1:2, :], 0.0), axis=1, keepdims=True)
+        shift = jnp.sum(jnp.where(eye, held[0, t, rows + 1 : rows + 2], 0.0), axis=1, keepdims=True)
         shift = jnp.broadcast_to(shift[0:rows], (rows, TILE)).astype(jnp.int32)
         shifts[t] = shift
         mark = jnp.where(lane >= shift, 1.0, 0.0)
@@ -177,13 +251,12 @@
         return c
 
     lax.fori_loop(0, n_f, prepare, 0)
-    received(1, held.at[0, pl.ds(0, n_f - 1)])
 
     def count_hits():
         index = iota((n_o * SUB, pair), 0)
-        place = (lax.div(index, SUB) * block + f * SUB + lax.rem(index, SUB)).astype(F32)
+        place = (lax.div(index, SUB) * block + mine * SUB + lax.rem(index, SUB)).astype(F32)
         chosen = jnp.concatenate(
-            [jnp.where(place == codes[t, 0:1, :], 1.0, 0.0).astype(BF16) for t in range(n_f)],
+            [jnp.where(place == held[0, t, rows : rows + 1], 1.0, 0.0).astype(BF16) for t in range(n_f)],
             axis=1,
         )
         hits = jnp.dot(chosen, marks[...], preferred_element_type=F32)
@@ -206,7 +279,7 @@
 
     def iteration(turn, c):
         def take_logs(t, total):
-            value = held[turn, t]
+            value = held[turn, t, 0:rows]
             at = pl.ds(pl.multiple_of(t * TILE, TILE), TILE)
             high, mid, low = split3(jnp.log(value + BACKGROUND))
             logs[0:rows, at] = high
@@ -257,7 +330,7 @@
         )
         num = num[:rows] + num[rows:]
         for t in range(n_f):
-            value = num[:, t * TILE : (t + 1) * TILE] + jnp.where(f == t, held[turn, t], 0.0)
+            value = num[:, t * TILE : (t + 1) * TILE] + jnp.where(f == t, held[turn, t, 0:rows], 0.0)
             shift = shifts[t]
             for k in range(7):
                 value = jnp.where((shift & (1 << k)) != 0, pltpu.roll(value, 1 << k, 1), value)
@@ -285,34 +358,31 @@
             for k in range(n_f):
                 part_out[turn, i * n_f + k] = part[k * SUB : (k + 1) * SUB]
 
-        def give(peer_o, peer_f):
-            copy(
-                7 + turn,
-                part_out.at[turn, peer_o * n_f + peer_f],
-                part_in.at[turn, me],
-                (peer_o, peer_f),
-            ).start()
-
-        def scatter(j, c):
-            peer = lax.rem(o + j, n_o)
+        def scatter(i, c):
+            peer = far_first(i)
             collect(peer)
 
-            def each(k, c):
-                give(peer, lax.rem(f + k, n_f))
+            def give(k, c):
+                at = chip_at(lax.div(k, 2))
+                side = lax.rem(core + k, 2)
+
+                @pl.when((peer != o) | (at * 2 + side != f))
+                def _():
+                    deliver(
+                        part_out.at[turn, peer * n_f + side * half + at],
+                        part_in.at[turn, me],
+                        send_sem.at[7 + turn],
+                        recv_sem.at[7 + turn],
+                        (peer, at * 2 + side),
+                    ).start()
+
                 return c
 
-            lax.fori_loop(0, n_f, each, 0)
-            return c
-
-        lax.fori_loop(1, n_o, scatter, 0)
-        collect(o)
-
-        def each(k, c):
-            give(o, lax.rem(f + k, n_f))
-            return c
-
-        lax.fori_loop(1, n_f, each, 0)
-        part_in[turn, me] = part_out[turn, me]
+            lax.fori_loop(0, n_f, give, 0)
+            return c
+
+        lax.fori_loop(0, n_o, scatter, 0)
+        part_in[turn, me] = part_out[turn, o * n_f + mine]
 
         @pl.when(turn == 0)
         def _():
@@ -322,29 +392,75 @@
         received(7 + turn, part_in.at[turn, pl.ds(0, n - 1)])
         brick = jnp.sum(part_in[turn], axis=0) / jnp.maximum(hits, 1.0)
         out_ref[...] = brick
-        volume[turn, me] = brick
-
-        def spread_out(j, c):
-            peer = lax.rem(me + j, n)
-            copy(
-                9 + turn,
-                volume.at[turn, me],
-                volume.at[turn, me],
-                (lax.div(peer, n_f), lax.rem(peer, n_f)),
+        slot = o * n_f + mine
+        volume[turn, slot] = brick
+
+        def spread_out(i, c):
+            peer = far_first(i)
+
+            def give(k, c):
+                at = chip_at(k)
+
+                @pl.when((peer != o) | (at != chip))
+                def _():
+                    deliver(
+                        volume.at[turn, slot],
+                        volume.at[turn, slot],
+                        send_sem.at[9 + turn],
+                        wide_recv.at[turn, o],
+                        (peer, at * 2 + core),
+                    ).start()
+
+                return c
+
+            return lax.fori_loop(0, half, give, c)
+
+        lax.fori_loop(0, n_o, spread_out, 0)
+
+        def relay(i, c):
+            peer = far_first(n_o - 1 - i)
+
+            @pl.when(peer == o)
+            def _():
+                few = volume.at[turn, pl.ds(0, half - 1)]
+                deliver(
+                    few, few, send_sem.at[9 + turn], wide_recv.at[turn, peer], (o, sibling)
+                ).wait_recv()
+
+            bricks = volume.at[turn, pl.ds(peer * n_f + core * half, half)]
+
+            @pl.when(peer != o)
+            def _():
+                deliver(
+                    bricks, bricks, send_sem.at[9 + turn], wide_recv.at[turn, peer], (o, sibling)
+                ).wait_recv()
+
+            deliver(
+                bricks, bricks, send_sem.at[11 + turn], wide_pass.at[turn, peer], (o, sibling)
             ).start()
             return c
 
-        lax.fori_loop(1, n, spread_out, 0)
-        received(9 + turn, volume.at[turn, pl.ds(0, n - 1)])
-        high, low = split2(volume[turn].reshape(places, TILE))
-        spread[:, :TILE] = high
-        spread[:, TILE:] = low
+        lax.fori_loop(0, n_o, relay, 0)
+
+        def land(i, c):
+            peer = far_first(n_o - 1 - i)
+            bricks = volume.at[turn, pl.ds(peer * n_f + (1 - core) * half, half)]
+            deliver(
+                bricks, bricks, send_sem.at[11 + turn], wide_pass.at[turn, peer], (o, sibling)
+            ).wait_recv()
+            here = pl.ds(pl.multiple_of(peer * block, block), block)
+            high, low = split2(volume[turn, pl.ds(peer * n_f, n_f)].reshape(block, TILE))
+            spread[here, :TILE] = high
+            spread[here, TILE:] = low
+            return c
+
+        lax.fori_loop(0, n_o, land, 0)
 
         @pl.when(turn < ITERS - 1)
         def _():
             def fill(t, c):
                 for k in range(4):
-                    held[turn + 1, t * 4 + k] = expand(t * 4 + k)
+                    held[turn + 1, t * 4 + k, 0:rows] = expand(t * 4 + k)
                 return c
 
             lax.fori_loop(0, n_f // 4, fill, 0)
@@ -354,14 +470,15 @@
     lax.fori_loop(0, ITERS, iteration, 0)
     new_ref[...] = expand(f)
 
-    sent(0, codes.at[pl.ds(0, n_f - 1)])
-    sent(1, held.at[0, pl.ds(0, n_f - 1)])
+    sent(0, held.at[0, pl.ds(0, half - 1)])
+    sent(1, held.at[0, pl.ds(0, half)])
     sent(2, hits_out.at[pl.ds(0, n_o - 1)])
     for turn in range(ITERS):
         sent(3 + turn, stats.at[turn, pl.ds(0, n_o - 1)])
         sent(5 + turn, dens.at[turn, pl.ds(0, n_f - 1)])
         sent(7 + turn, part_out.at[turn, pl.ds(0, n - 1)])
-        sent(9 + turn, volume.at[turn, pl.ds(0, n - 1)])
+        sent(9 + turn, volume.at[turn, pl.ds(0, n_o * half - 1)])
+        sent(11 + turn, volume.at[turn, pl.ds(0, n_o * half)])
 
 
 def on_device(n_o, n_f, slices, counts, fluence, tile_brick, tile_base):
@@ -370,17 +487,6 @@
     pair = 2 * rows
     block = n_f * SUB
     places = n_o * block
-    code = tile_brick[:, :, 0] * VOX + tile_base
-    place = code // TILE
-    shift = code % TILE
-    codes = jnp.concatenate(
-        [
-            jnp.concatenate([place, place + 1], axis=1),
-            jnp.concatenate([shift, shift], axis=1),
-            jnp.zeros((SUB - 2, pair), jnp.int32),
-        ],
-        axis=0,
-    ).astype(F32)
     vmem = pl.BlockSpec(memory_space=pltpu.VMEM)
     new, brick = pl.pallas_call(
         functools.partial(kernel, n_o, n_f),
@@ -388,14 +494,13 @@
             jax.ShapeDtypeStruct((rows, TILE), F32),
             jax.ShapeDtypeStruct((SUB, TILE), F32),
         ),
-        in_specs=[vmem, vmem, vmem, pl.BlockSpec(memory_space=pl.ANY)],
+        in_specs=[vmem, vmem, vmem, vmem, pl.BlockSpec(memory_space=pl.ANY)],
         out_specs=(vmem, vmem),
         scratch_shapes=[
             pltpu.VMEM((frames, pixels), F32),
             pltpu.VMEM((frames, pixels), BF16),
             pltpu.VMEM((frames, pixels), BF16),
-            pltpu.VMEM((ITERS, n_f, rows, TILE), F32),
-            pltpu.VMEM((n_f, SUB, pair), F32),
+            pltpu.VMEM((ITERS, n_f, rows + SUB, TILE), F32),
             pltpu.VMEM((ITERS, n_o, 2 * (frames // TILE), TILE), F32),
             pltpu.VMEM((ITERS, n_f, 1, TILE), F32),
             pltpu.VMEM((places, n_f * pair), BF16),
@@ -412,13 +517,17 @@
             pltpu.VMEM((n_o, SUB, TILE), F32),
             pltpu.VMEM((n_o, SUB, TILE), F32),
             pltpu.SemaphoreType.DMA((LOAD,)),
-            pltpu.SemaphoreType.DMA((3 + 4 * ITERS,)),
-            pltpu.SemaphoreType.DMA((3 + 4 * ITERS,)),
+            pltpu.SemaphoreType.DMA((3 + 5 * ITERS,)),
+            pltpu.SemaphoreType.DMA((3 + 5 * ITERS,)),
+            pltpu.SemaphoreType.DMA((n_f // 2,)),
+            pltpu.SemaphoreType.DMA((n_f // 2,)),
+            pltpu.SemaphoreType.DMA((ITERS, n_o)),
+            pltpu.SemaphoreType.DMA((ITERS, n_o)),
         ],
         compiler_params=pltpu.CompilerParams(
             collective_id=0, has_side_effects=True, vmem_limit_bytes=60 << 20
         ),
-    )(slices, codes, fluence[None, :], counts)
+    )(slices, tile_brick[:, :, 0], tile_base, fluence[None, :], counts)
     return new, brick.reshape(1, SUB * TILE)
 
 

time: 94.7 us -> 90.4 us (0.955)
  Pallas kernels: 89.7 us -> 86.8 us
  other arithmetic: 1.36 us -> 0 us
    pallas_call x1, Pallas kernels: 89.7 us -> 86.8 us  [on_device(): pl.pallas_call(functools.partial(kernel, n_o, n_f), out_shape=(jax.ShapeD...]
where the time goes in v3:
time: 90.4 us; the launch traced here: 90.1 us
  Pallas kernels  86.8 us (96%)
  local copies, waits for them, and re-layouts  2.65 us (3%)
    pallas_call x1, Pallas kernels, on_device(): pl.pallas_call(functools.partial(kernel, n_o, n_f), out_shape=(jax.ShapeD...  86.8 us
    unnamed x2, local copies, waits for them, and re-layouts  2.65 us

profile of v3, /device:TPU:1, one launch (start us, length us, event | category | flops | bytes accessed | tf_op | source)
XLA Modules:
  0.0 90.1 jit_solution(6573670630362578633)
XLA Ops:
  0.6 86.8 %shard_map.68 = (f32[64,128]{1,0:T(8,128)}, f32[8,128]{1,0:T(8,128)}) custom-call(f32[64,128]{1,0:T(8,128)} %slices_ref.1, s32[1,64]{1,0:T(1,128)} %bitcast.5, s32[1,64]{1,0:T(1,128)} %base_ref.1, f32[1,512]{1,0:T(1,128)} %bitcast.4, f32[512,2048]{1,0:T(8,128)} %counts_ref.1), custom_call_target="tpu_custom_call" | custom-call | tf_op jit(solution)/shard_map/pallas_call | solution.py:491
  87.5 1.4 %copy.9 = f32[64,128]{1,0:T(8,128)} copy(f32[64,128]{1,0:T(8,128)} %get-tuple-element.8) | data formatting | bytes 65536
  88.9 1.3 %copy.10 = f32[1,1024]{1,0:T(1,128)} copy(f32[1,1024]{1,0:T(1,128)} %bitcast.3) | data formatting | bytes 8192

commit v4 on v3

--- a/solution.py
+++ b/solution.py
@@ -90,24 +90,35 @@
     mine = core * half + chip
     lane = iota((rows, TILE), 1)
 
-    barrier = pltpu.get_barrier_semaphore()
-
-    def greet(j, c):
-        peer = lax.rem(me + j, n)
-        pl.semaphore_signal(
-            barrier,
-            inc=1,
-            device_id=(lax.div(peer, n_f), lax.rem(peer, n_f)),
-            device_id_type=MESH,
-        )
-        return c
-
-    lax.fori_loop(1, n, greet, 0)
+    near = lambda d, size: min(d, size - d)
+    turns_o = sorted(range(n_o), key=lambda d: -near(d, n_o))
+    turns_f = sorted(
+        ((x, y, c) for x in range(ring) for y in range(2) for c in range(2)),
+        key=lambda d: -(4 * near(d[0], ring) + 4 * d[1] + d[2]),
+    )
+    peers_o = [lax.rem(o + d, n_o) for d in turns_o]
+    chip_x, chip_y = lax.div(chip, 2), lax.rem(chip, 2)
+    chips = [
+        lax.rem(chip_x + x, ring) * 2 + lax.rem(chip_y + y, 2) for x, y, c in turns_f
+    ]
+    sides = [lax.rem(core + c, 2) for x, y, c in turns_f]
+    peers_f = [at * 2 + side for at, side in zip(chips, sides)]
+    slots_f = [side * half + at for at, side in zip(chips, sides)]
+    here_f = turns_f.index((0, 0, 0))
+    same_core = [k for k in range(n_f) if turns_f[k][2] == 0]
+
     step = frames // LOAD
     for i in range(LOAD):
         pltpu.make_async_copy(
             counts_ref.at[pl.ds(i * step, step)], raw.at[pl.ds(i * step, step)], load_sem.at[i]
         ).start()
+    barrier = pltpu.get_barrier_semaphore()
+    for i in range(n_o):
+        for k in range(n_f):
+            if turns_o[i] != 0 or k != here_f:
+                pl.semaphore_signal(
+                    barrier, inc=1, device_id=(peers_o[i], peers_f[k]), device_id_type=MESH
+                )
 
     held[0, f, 0:rows] = slices_ref[...]
     named = brick_ref[...]
@@ -170,13 +181,6 @@
     def sent(which, whole):
         copy(which, whole, whole, (lax.rem(o + 1, n_o), f)).wait_send()
 
-    def chip_at(k):
-        x = lax.rem(lax.div(chip, 2) + lax.div(k, 2) + ring // 2, ring)
-        return x * 2 + lax.rem(chip + 1 + k, 2)
-
-    def far_first(i):
-        return lax.rem(o + n_o // 2 + (1 - 2 * lax.rem(i, 2)) * lax.div(i + 1, 2), n_o)
-
     def deliver(src, dst, out, into, to):
         return pltpu.make_async_remote_copy(
             src_ref=src,
@@ -191,66 +195,53 @@
         packet = held.at[0, at * 2 + core]
         deliver(packet, packet, send_sem.at[1], first_pass.at[at], (o, sibling)).start()
 
-    def send_first(k, c):
-        at = chip_at(k)
-
-        @pl.when(at != chip)
-        def _():
-            packet = held.at[0, f]
-            deliver(
-                packet, packet, send_sem.at[0], first_recv.at[chip], (o, at * 2 + core)
-            ).start()
-
-        return c
-
-    lax.fori_loop(0, half, send_first, 0)
+    away = [k for k in same_core if k != here_f]
+    for k in away:
+        packet = held.at[0, f]
+        deliver(packet, packet, send_sem.at[0], first_recv.at[chip], (o, peers_f[k])).start()
     pass_first(chip)
-
-    def relay_first(k, c):
-        at = chip_at(half - 1 - k)
-
-        @pl.when(at != chip)
-        def _():
-            packet = held.at[0, at * 2 + core]
-            deliver(packet, packet, send_sem.at[0], first_recv.at[at], (o, sibling)).wait_recv()
-            pass_first(at)
-
-        return c
-
-    lax.fori_loop(0, half, relay_first, 0)
-
-    def land_first(k, c):
-        at = chip_at(half - 1 - k)
-        packet = held.at[0, at * 2 + 1 - core]
-        deliver(packet, packet, send_sem.at[1], first_pass.at[at], (o, sibling)).wait_recv()
-        return c
-
-    lax.fori_loop(0, half, land_first, 0)
+    for k in reversed(away):
+        packet = held.at[0, peers_f[k]]
+        into = first_recv.at[chips[k]]
+        deliver(packet, packet, send_sem.at[0], into, (o, sibling)).wait_recv()
+        pass_first(chips[k])
+    for k in reversed(same_core):
+        packet = held.at[0, chips[k] * 2 + 1 - core]
+        into = first_pass.at[chips[k]]
+        deliver(packet, packet, send_sem.at[1], into, (o, sibling)).wait_recv()
     diagonal = iota((rows, TILE), 0) == lane
     eye = iota((pair, pair), 0) == iota((pair, pair), 1)
 
-    def prepare(t, c):
+    def prepare_to(t):
         row = held[0, t, rows : rows + 1]
         at = pl.ds(pl.multiple_of(t * pair, pair), pair)
-
-        def fill(i, c):
-            here = pl.ds(pl.multiple_of(i * block, block), block)
+        for i in range(n_o):
             place = (iota((block, pair), 0) + i * block).astype(F32)
-            gather_to[here, at] = jnp.where(place == row, 1.0, 0.0).astype(BF16)
-            return c
-
-        lax.fori_loop(0, n_o, fill, 0)
-        column = jnp.sum(jnp.where(eye, row, 0.0), axis=1, keepdims=True)
-        place = iota((pair, places), 1).astype(F32)
-        gather_from[at, :] = jnp.where(place == column, 1.0, 0.0).astype(BF16)
-        shift = jnp.sum(jnp.where(eye, held[0, t, rows + 1 : rows + 2], 0.0), axis=1, keepdims=True)
+            gather_to[i * block : (i + 1) * block, at] = jnp.where(
+                place == row, 1.0, 0.0
+            ).astype(BF16)
+        shift = jnp.sum(
+            jnp.where(eye, held[0, t, rows + 1 : rows + 2], 0.0), axis=1, keepdims=True
+        )
         shift = jnp.broadcast_to(shift[0:rows], (rows, TILE)).astype(jnp.int32)
         shifts[t] = shift
         mark = jnp.where(lane >= shift, 1.0, 0.0)
         marks[at, :] = jnp.concatenate([mark, 1.0 - mark], axis=0).astype(BF16)
-        return c
-
-    lax.fori_loop(0, n_f, prepare, 0)
+
+    def prepare_from(t):
+        row = held[0, t, rows : rows + 1]
+        at = pl.ds(pl.multiple_of(t * pair, pair), pair)
+        column = jnp.sum(jnp.where(eye, row, 0.0), axis=1, keepdims=True)
+        place = iota((pair, places), 1).astype(F32)
+        gather_from[at, :] = jnp.where(place == column, 1.0, 0.0).astype(BF16)
+
+    def by_twos(work):
+        def body(t, c):
+            work(t * 2)
+            work(t * 2 + 1)
+            return c
+
+        lax.fori_loop(0, n_f // 2, body, 0)
 
     def count_hits():
         index = iota((n_o * SUB, pair), 0)
@@ -306,6 +297,7 @@
 
         @pl.when(turn == 0)
         def _():
+            by_twos(prepare_to)
             count_hits()
 
         received(3 + turn, stats.at[turn, pl.ds(0, n_o - 1)])
@@ -335,6 +327,11 @@
             for k in range(7):
                 value = jnp.where((shift & (1 << k)) != 0, pltpu.roll(value, 1 << k, 1), value)
             moved[t] = value
+
+        @pl.when(turn == 0)
+        def _():
+            by_twos(prepare_from)
+
         received(5 + turn, dens.at[turn, pl.ds(0, n_f - 1)])
         weight = dens[turn, 0]
         for i in range(1, n_f):
@@ -358,30 +355,22 @@
             for k in range(n_f):
                 part_out[turn, i * n_f + k] = part[k * SUB : (k + 1) * SUB]
 
-        def scatter(i, c):
-            peer = far_first(i)
-            collect(peer)
-
-            def give(k, c):
-                at = chip_at(lax.div(k, 2))
-                side = lax.rem(core + k, 2)
-
-                @pl.when((peer != o) | (at * 2 + side != f))
-                def _():
+        def give(i):
+            for k in range(n_f):
+                if turns_o[i] != 0 or k != here_f:
                     deliver(
-                        part_out.at[turn, peer * n_f + side * half + at],
+                        part_out.at[turn, peers_o[i] * n_f + slots_f[k]],
                         part_in.at[turn, me],
                         send_sem.at[7 + turn],
                         recv_sem.at[7 + turn],
-                        (peer, at * 2 + side),
+                        (peers_o[i], peers_f[k]),
                     ).start()
 
-                return c
-
-            lax.fori_loop(0, n_f, give, 0)
-            return c
-
-        lax.fori_loop(0, n_o, scatter, 0)
+        for i in range(n_o):
+            collect(peers_o[i])
+            if i > 0:
+                give(i - 1)
+        give(n_o - 1)
         part_in[turn, me] = part_out[turn, o * n_f + mine]
 
         @pl.when(turn == 0)
@@ -395,55 +384,30 @@
         slot = o * n_f + mine
         volume[turn, slot] = brick
 
-        def spread_out(i, c):
-            peer = far_first(i)
-
-            def give(k, c):
-                at = chip_at(k)
-
-                @pl.when((peer != o) | (at != chip))
-                def _():
+        for i in range(n_o):
+            for k in same_core:
+                if turns_o[i] != 0 or k != here_f:
                     deliver(
                         volume.at[turn, slot],
                         volume.at[turn, slot],
                         send_sem.at[9 + turn],
                         wide_recv.at[turn, o],
-                        (peer, at * 2 + core),
+                        (peers_o[i], peers_f[k]),
                     ).start()
 
-                return c
-
-            return lax.fori_loop(0, half, give, c)
-
-        lax.fori_loop(0, n_o, spread_out, 0)
-
-        def relay(i, c):
-            peer = far_first(n_o - 1 - i)
-
-            @pl.when(peer == o)
-            def _():
-                few = volume.at[turn, pl.ds(0, half - 1)]
-                deliver(
-                    few, few, send_sem.at[9 + turn], wide_recv.at[turn, peer], (o, sibling)
-                ).wait_recv()
-
+        for i in reversed(range(n_o)):
+            peer = peers_o[i]
+            count = half if turns_o[i] != 0 else half - 1
+            some = volume.at[turn, pl.ds(peer * n_f + core * half, count)]
+            deliver(
+                some, some, send_sem.at[9 + turn], wide_recv.at[turn, peer], (o, sibling)
+            ).wait_recv()
             bricks = volume.at[turn, pl.ds(peer * n_f + core * half, half)]
-
-            @pl.when(peer != o)
-            def _():
-                deliver(
-                    bricks, bricks, send_sem.at[9 + turn], wide_recv.at[turn, peer], (o, sibling)
-                ).wait_recv()
-
             deliver(
                 bricks, bricks, send_sem.at[11 + turn], wide_pass.at[turn, peer], (o, sibling)
             ).start()
-            return c
-
-        lax.fori_loop(0, n_o, relay, 0)
-
-        def land(i, c):
-            peer = far_first(n_o - 1 - i)
+        for i in reversed(range(n_o)):
+            peer = peers_o[i]
             bricks = volume.at[turn, pl.ds(peer * n_f + (1 - core) * half, half)]
             deliver(
                 bricks, bricks, send_sem.at[11 + turn], wide_pass.at[turn, peer], (o, sibling)
@@ -452,9 +416,6 @@
             high, low = split2(volume[turn, pl.ds(peer * n_f, n_f)].reshape(block, TILE))
             spread[here, :TILE] = high
             spread[here, TILE:] = low
-            return c
-
-        lax.fori_loop(0, n_o, land, 0)
 
         @pl.when(turn < ITERS - 1)
         def _():

time: 90.4 us -> 84.9 us (0.939)
  Pallas kernels: 86.8 us -> 81.4 us
    pallas_call x1, Pallas kernels: 86.8 us -> 81.4 us  [on_device(): pl.pallas_call(functools.partial(kernel, n_o, n_f), out_shape=(jax.ShapeD...]
where the time goes in v4:
time: 84.9 us; the launch traced here: 84.7 us
  Pallas kernels  81.4 us (96%)
  local copies, waits for them, and re-layouts  2.65 us (3%)
    pallas_call x1, Pallas kernels, on_device(): pl.pallas_call(functools.partial(kernel, n_o, n_f), out_shape=(jax.ShapeD...  81.4 us
    unnamed x2, local copies, waits for them, and re-layouts  2.65 us

profile of v4, /device:TPU:1, one launch (start us, length us, event | category | flops | bytes accessed | tf_op | source)
XLA Modules:
  0.0 84.7 jit_solution(9317646813956217844)
XLA Ops:
  0.6 81.4 %shard_map.68 = (f32[64,128]{1,0:T(8,128)}, f32[8,128]{1,0:T(8,128)}) custom-call(f32[64,128]{1,0:T(8,128)} %slices_ref.1, s32[1,64]{1,0:T(1,128)} %bitcast.5, s32[1,64]{1,0:T(1,128)} %base_ref.1, f32[1,512]{1,0:T(1,128)} %bitcast.4, f32[512,2048]{1,0:T(8,128)} %counts_ref.1), custom_call_target="tpu_custom_call" | custom-call | tf_op jit(solution)/shard_map/pallas_call | solution.py:452
  82.0 1.4 %copy.9 = f32[64,128]{1,0:T(8,128)} copy(f32[64,128]{1,0:T(8,128)} %get-tuple-element.8) | data formatting | bytes 65536
  83.4 1.3 %copy.10 = f32[1,1024]{1,0:T(1,128)} copy(f32[1,1024]{1,0:T(1,128)} %bitcast.3) | data formatting | bytes 8192

commit v5 on v4

--- a/solution.py
+++ b/solution.py
@@ -48,6 +48,8 @@
     raw,
     count_high,
     count_low,
+    count_high_t,
+    count_low_t,
     held,
     stats,
     dens,
@@ -59,6 +61,8 @@
     marks,
     logs,
     part_out,
+    pair_in,
+    paired,
     part_in,
     volume,
     spread,
@@ -69,6 +73,7 @@
     recv_sem,
     first_recv,
     first_pass,
+    pair_recv,
     wide_recv,
     wide_pass,
 ):
@@ -90,22 +95,42 @@
     mine = core * half + chip
     lane = iota((rows, TILE), 1)
 
-    near = lambda d, size: min(d, size - d)
-    turns_o = sorted(range(n_o), key=lambda d: -near(d, n_o))
+    def near(d, size):
+        return min(d, size - d)
+
+    depth = n_o // 2
+    turns_o = sorted(
+        ((z, y) for z in range(depth) for y in range(2)), key=lambda d: -near(d[0], depth) - d[1]
+    )
     turns_f = sorted(
         ((x, y, c) for x in range(ring) for y in range(2) for c in range(2)),
-        key=lambda d: -(4 * near(d[0], ring) + 4 * d[1] + d[2]),
-    )
-    peers_o = [lax.rem(o + d, n_o) for d in turns_o]
+        key=lambda d: -(4 * near(d[0], ring) + 8 * d[1] + d[2]),
+    )
+    at_z, at_y = lax.div(o, 2), lax.rem(o, 2)
+    peers_o = [lax.rem(at_z + z, depth) * 2 + lax.rem(at_y + y, 2) for z, y in turns_o]
     chip_x, chip_y = lax.div(chip, 2), lax.rem(chip, 2)
     chips = [
         lax.rem(chip_x + x, ring) * 2 + lax.rem(chip_y + y, 2) for x, y, c in turns_f
     ]
     sides = [lax.rem(core + c, 2) for x, y, c in turns_f]
     peers_f = [at * 2 + side for at, side in zip(chips, sides)]
-    slots_f = [side * half + at for at, side in zip(chips, sides)]
-    here_f = turns_f.index((0, 0, 0))
+    here_o, here_f = turns_o.index((0, 0)), turns_f.index((0, 0, 0))
     same_core = [k for k in range(n_f) if turns_f[k][2] == 0]
+
+    def hops(i, k):
+        (z, low), (x, high, c) = turns_o[i], turns_f[k]
+        return near(z, depth) + near(x, ring) + ((0, 1), (2, 1))[high][low]
+
+    pairs = sorted(
+        ((i, k) for i in range(n_o) for k in same_core), key=lambda d: -hops(*d)
+    )
+    far = hops(*pairs[0]) - 1
+    others = [d for d in pairs if d != (here_o, here_f)]
+
+    def is_peer(i, k):
+        if (i, k) == (here_o, here_f):
+            return False
+        return k in same_core or i == here_o or hops(i, k) >= far
 
     step = frames // LOAD
     for i in range(LOAD):
@@ -113,12 +138,11 @@
             counts_ref.at[pl.ds(i * step, step)], raw.at[pl.ds(i * step, step)], load_sem.at[i]
         ).start()
     barrier = pltpu.get_barrier_semaphore()
-    for i in range(n_o):
-        for k in range(n_f):
-            if turns_o[i] != 0 or k != here_f:
-                pl.semaphore_signal(
-                    barrier, inc=1, device_id=(peers_o[i], peers_f[k]), device_id_type=MESH
-                )
+    peers = [(i, k) for i in range(n_o) for k in range(n_f) if is_peer(i, k)]
+    for i, k in sorted(peers, key=lambda d: -hops(*d)):
+        pl.semaphore_signal(
+            barrier, inc=1, device_id=(peers_o[i], peers_f[k]), device_id_type=MESH
+        )
 
     held[0, f, 0:rows] = slices_ref[...]
     named = brick_ref[...]
@@ -133,21 +157,24 @@
     held[0, f, rows + 1 : rows + 2] = jnp.concatenate([shift, shift], axis=1).astype(F32)
     held[0, f, rows + 2 : rows + SUB] = jnp.zeros((SUB - 2, TILE), F32)
 
+    def load(i):
+        here = pl.ds(i * step, step)
+        pltpu.make_async_copy(counts_ref.at[here], raw.at[here], load_sem.at[i]).wait()
+
+        def convert(j, c):
+            at = pl.ds(pl.multiple_of(j * TILE, TILE), TILE)
+            high, low = split2(raw[here, at])
+            count_high[here, at] = high
+            count_low[here, at] = low
+            count_high_t[at, here] = high.T
+            count_low_t[at, here] = low.T
+            return c
+
+        lax.fori_loop(0, n_f, convert, 0)
+
     for i in range(LOAD):
-        pltpu.make_async_copy(
-            counts_ref.at[pl.ds(i * step, step)], raw.at[pl.ds(i * step, step)], load_sem.at[i]
-        ).wait()
-
-        def convert(j, c):
-            at = pl.ds(pl.multiple_of(i * step + j * 16, 16), 16)
-            high, low = split2(raw[at, :])
-            count_high[at, :] = high
-            count_low[at, :] = low
-            return c
-
-        lax.fori_loop(0, step // 16, convert, 0)
-
-    pl.semaphore_wait(barrier, n - 1)
+        load(i)
+    pl.semaphore_wait(barrier, len(peers))
 
     def copy(which, src, dst, to):
         return pltpu.make_async_remote_copy(
@@ -216,7 +243,7 @@
         row = held[0, t, rows : rows + 1]
         at = pl.ds(pl.multiple_of(t * pair, pair), pair)
         for i in range(n_o):
-            place = (iota((block, pair), 0) + i * block).astype(F32)
+            place = (iota((block, pair), 0) + peers_o[i] * block).astype(F32)
             gather_to[i * block : (i + 1) * block, at] = jnp.where(
                 place == row, 1.0, 0.0
             ).astype(BF16)
@@ -256,17 +283,24 @@
         send_orient(2, lambda peer: hits_out.at[peer], hits_in.at[o])
         hits_in[o] = hits_out[o]
 
-    def expand(t):
-        at = pl.ds(pl.multiple_of(t * pair, pair), pair)
+    def expand(t, many):
+        at = pl.ds(t * pair if many > 1 else pl.multiple_of(t * pair, pair), many * pair)
         found = jnp.dot(gather_from[at, :], spread[...], preferred_element_type=F32)
         found = found[:, :TILE] + found[:, TILE:]
-        shift = shifts[t]
-        value = jnp.where(lane >= shift, found[:rows], found[rows:])
-        for k in range(7):
+        values = []
+        for i in range(many):
+            shift = shifts[t + i]
             value = jnp.where(
-                (shift & (1 << k)) != 0, pltpu.roll(value, TILE - (1 << k), 1), value
+                lane >= shift,
+                found[i * pair : i * pair + rows],
+                found[i * pair + rows : (i + 1) * pair],
             )
-        return value
+            for k in range(7):
+                value = jnp.where(
+                    (shift & (1 << k)) != 0, pltpu.roll(value, TILE - (1 << k), 1), value
+                )
+            values.append(value)
+        return values
 
     def iteration(turn, c):
         def take_logs(t, total):
@@ -280,10 +314,9 @@
 
         total = lax.fori_loop(0, n_f, take_logs, jnp.zeros((rows, TILE), F32))
         total = jnp.sum(total, axis=1, keepdims=True)
-        across = (((1,), (1,)), ((), ()))
-        like = lax.dot_general(
-            logs[...], count_high[...], across, preferred_element_type=F32
-        ) + lax.dot_general(logs[...], count_low[...], across, preferred_element_type=F32)
+        like = jnp.dot(logs[...], count_high_t[...], preferred_element_type=F32) + jnp.dot(
+            logs[...], count_low_t[...], preferred_element_type=F32
+        )
         like = like[:rows] + like[rows : 2 * rows] + like[2 * rows :]
         score = SHARPNESS * (like - total * fluence_ref[...])
         top = jnp.max(score, axis=0, keepdims=True)
@@ -348,88 +381,104 @@
             tiles[at + rows : at + pair, :TILE] = jnp.where(first, none, high)
             tiles[at + rows : at + pair, TILE:] = jnp.where(first, none, low)
 
-        def collect(i):
-            here = pl.ds(pl.multiple_of(i * block, block), block)
+        groups = min(4, n_o)
+        group = n_o // groups
+
+        def product(g):
+            here = slice(g * group * block, (g + 1) * group * block)
             part = jnp.dot(gather_to[here, :], tiles[...], preferred_element_type=F32)
-            part = part[:, :TILE] + part[:, TILE:]
-            for k in range(n_f):
-                part_out[turn, i * n_f + k] = part[k * SUB : (k + 1) * SUB]
-
-        def give(i):
-            for k in range(n_f):
-                if turns_o[i] != 0 or k != here_f:
-                    deliver(
-                        part_out.at[turn, peers_o[i] * n_f + slots_f[k]],
-                        part_in.at[turn, me],
-                        send_sem.at[7 + turn],
-                        recv_sem.at[7 + turn],
-                        (peers_o[i], peers_f[k]),
-                    ).start()
-
-        for i in range(n_o):
-            collect(peers_o[i])
-            if i > 0:
-                give(i - 1)
-        give(n_o - 1)
-        part_in[turn, me] = part_out[turn, o * n_f + mine]
+            part = (part[:, :TILE] + part[:, TILE:]).reshape(group, 2, half, SUB, TILE)
+            for j in range(group):
+                i = g * group + j
+                for side in range(2):
+                    part_out[turn, side, i] = part[j, side]
+                deliver(
+                    part_out.at[turn, 1 - core, i],
+                    pair_in.at[turn, i],
+                    send_sem.at[13 + turn],
+                    pair_recv.at[turn, i],
+                    (o, sibling),
+                ).start()
+
+        def release(g):
+            for i in range(g * group, (g + 1) * group):
+                into = pair_recv.at[turn, i]
+                got = pair_in.at[turn, i]
+                deliver(got, got, send_sem.at[13 + turn], into, (o, sibling)).wait_recv()
+                paired[turn, i] = part_out[turn, core, i] + pair_in[turn, i]
+                for k in same_core:
+                    if (i, k) != (here_o, here_f):
+                        deliver(
+                            paired.at[turn, i, chips[k]],
+                            part_in.at[turn, o * half + chip],
+                            send_sem.at[7 + turn],
+                            recv_sem.at[7 + turn],
+                            (peers_o[i], peers_f[k]),
+                        ).start()
+
+        for g in range(groups):
+            product(g)
+            if g >= 2:
+                release(g - 2)
+        for g in range(max(0, groups - 2), groups):
+            release(g)
+        part_in[turn, o * half + chip] = paired[turn, n_o - 1, chip]
 
         @pl.when(turn == 0)
         def _():
             received(2, hits_in.at[pl.ds(0, n_o - 1)])
 
         hits = jnp.sum(hits_in[...], axis=0)
-        received(7 + turn, part_in.at[turn, pl.ds(0, n - 1)])
+        received(7 + turn, part_in.at[turn, pl.ds(0, n // 2 - 1)])
         brick = jnp.sum(part_in[turn], axis=0) / jnp.maximum(hits, 1.0)
         out_ref[...] = brick
         slot = o * n_f + mine
         volume[turn, slot] = brick
 
-        for i in range(n_o):
-            for k in same_core:
-                if turns_o[i] != 0 or k != here_f:
-                    deliver(
-                        volume.at[turn, slot],
-                        volume.at[turn, slot],
-                        send_sem.at[9 + turn],
-                        wide_recv.at[turn, o],
-                        (peers_o[i], peers_f[k]),
-                    ).start()
-
-        for i in reversed(range(n_o)):
-            peer = peers_o[i]
-            count = half if turns_o[i] != 0 else half - 1
-            some = volume.at[turn, pl.ds(peer * n_f + core * half, count)]
+        for i, k in others:
+            brick_at = volume.at[turn, slot]
+            into = wide_recv.at[turn, o * half + chip]
             deliver(
-                some, some, send_sem.at[9 + turn], wide_recv.at[turn, peer], (o, sibling)
-            ).wait_recv()
-            bricks = volume.at[turn, pl.ds(peer * n_f + core * half, half)]
+                brick_at, brick_at, send_sem.at[9 + turn], into, (peers_o[i], peers_f[k])
+            ).start()
+            if hops(i, k) >= far:
+                across = (peers_o[i], chips[k] * 2 + 1 - core)
+                deliver(
+                    brick_at, brick_at, send_sem.at[9 + turn], wide_pass.at[turn], across
+                ).start()
+
+        def pass_on(at):
+            brick_at = volume.at[turn, at]
             deliver(
-                bricks, bricks, send_sem.at[11 + turn], wide_pass.at[turn, peer], (o, sibling)
+                brick_at, brick_at, send_sem.at[11 + turn], wide_pass.at[turn], (o, sibling)
             ).start()
-        for i in reversed(range(n_o)):
-            peer = peers_o[i]
-            bricks = volume.at[turn, pl.ds(peer * n_f + (1 - core) * half, half)]
-            deliver(
-                bricks, bricks, send_sem.at[11 + turn], wide_pass.at[turn, peer], (o, sibling)
-            ).wait_recv()
-            here = pl.ds(pl.multiple_of(peer * block, block), block)
-            high, low = split2(volume[turn, pl.ds(peer * n_f, n_f)].reshape(block, TILE))
-            spread[here, :TILE] = high
-            spread[here, TILE:] = low
+
+        pass_on(slot)
+        for i, k in reversed(others):
+            at = peers_o[i] * n_f + core * half + chips[k]
+            into = wide_recv.at[turn, peers_o[i] * half + chips[k]]
+            brick_at = volume.at[turn, at]
+            deliver(brick_at, brick_at, send_sem.at[9 + turn], into, (o, sibling)).wait_recv()
+            if hops(i, k) < far:
+                pass_on(at)
+        bricks = volume.at[turn, pl.ds(0, n_o * half)]
+        deliver(
+            bricks, bricks, send_sem.at[11 + turn], wide_pass.at[turn], (o, sibling)
+        ).wait_recv()
+        high, low = split2(volume[turn].reshape(places, TILE))
+        spread[:, :TILE] = high
+        spread[:, TILE:] = low
 
         @pl.when(turn < ITERS - 1)
         def _():
-            def fill(t, c):
-                for k in range(4):
-                    held[turn + 1, t * 4 + k, 0:rows] = expand(t * 4 + k)
-                return c
-
-            lax.fori_loop(0, n_f // 4, fill, 0)
+            for t in range(0, n_f, 4):
+                for k, value in enumerate(expand(t, 4)):
+                    held[turn + 1, t + k, 0:rows] = value
 
         return c
 
     lax.fori_loop(0, ITERS, iteration, 0)
-    new_ref[...] = expand(f)
+    new_ref[...] = expand(f, 1)[0]
 
     sent(0, held.at[0, pl.ds(0, half - 1)])
     sent(1, held.at[0, pl.ds(0, half)])
@@ -437,9 +486,16 @@
     for turn in range(ITERS):
         sent(3 + turn, stats.at[turn, pl.ds(0, n_o - 1)])
         sent(5 + turn, dens.at[turn, pl.ds(0, n_f - 1)])
-        sent(7 + turn, part_out.at[turn, pl.ds(0, n - 1)])
-        sent(9 + turn, volume.at[turn, pl.ds(0, n_o * half - 1)])
-        sent(11 + turn, volume.at[turn, pl.ds(0, n_o * half)])
+        sent(7 + turn, part_in.at[turn, pl.ds(0, n // 2 - 1)])
+        double = sum(hops(*d) >= far for d in others)
+        sent(9 + turn, volume.at[turn, pl.ds(0, n_o * half - 1 + double)])
+        sent(13 + turn, pair_in.at[turn])
+        sent(11 + turn, volume.at[turn, pl.ds(0, n_o * half - double)])
+
+
+def hand_over(new_ref, brick_ref, new_out, brick_out):
+    new_out[...] = new_ref[...]
+    brick_out[...] = brick_ref[...]
 
 
 def on_device(n_o, n_f, slices, counts, fluence, tile_brick, tile_base):
@@ -449,18 +505,21 @@
     block = n_f * SUB
     places = n_o * block
     vmem = pl.BlockSpec(memory_space=pltpu.VMEM)
-    new, brick = pl.pallas_call(
+    shapes = (
+        jax.ShapeDtypeStruct((rows, TILE), F32),
+        jax.ShapeDtypeStruct((SUB, TILE), F32),
+    )
+    both = pl.pallas_call(
         functools.partial(kernel, n_o, n_f),
-        out_shape=(
-            jax.ShapeDtypeStruct((rows, TILE), F32),
-            jax.ShapeDtypeStruct((SUB, TILE), F32),
-        ),
+        out_shape=shapes,
         in_specs=[vmem, vmem, vmem, vmem, pl.BlockSpec(memory_space=pl.ANY)],
         out_specs=(vmem, vmem),
         scratch_shapes=[
             pltpu.VMEM((frames, pixels), F32),
             pltpu.VMEM((frames, pixels), BF16),
             pltpu.VMEM((frames, pixels), BF16),
+            pltpu.VMEM((pixels, frames), BF16),
+            pltpu.VMEM((pixels, frames), BF16),
             pltpu.VMEM((ITERS, n_f, rows + SUB, TILE), F32),
             pltpu.VMEM((ITERS, n_o, 2 * (frames // TILE), TILE), F32),
             pltpu.VMEM((ITERS, n_f, 1, TILE), F32),
@@ -471,24 +530,33 @@
             pltpu.VMEM((n_f * pair, 2 * TILE), BF16),
             pltpu.VMEM((n_f * pair, TILE), BF16),
             pltpu.VMEM((3 * rows, pixels), BF16),
-            pltpu.VMEM((ITERS, n_o * n_f, SUB, TILE), F32),
-            pltpu.VMEM((ITERS, n_o * n_f, SUB, TILE), F32),
+            pltpu.VMEM((ITERS, 2, n_o, n_f // 2, SUB, TILE), F32),
+            pltpu.VMEM((ITERS, n_o, n_f // 2, SUB, TILE), F32),
+            pltpu.VMEM((ITERS, n_o, n_f // 2, SUB, TILE), F32),
+            pltpu.VMEM((ITERS, n_o * n_f // 2, SUB, TILE), F32),
             pltpu.VMEM((ITERS, n_o * n_f, SUB, TILE), F32),
             pltpu.VMEM((places, 2 * TILE), BF16),
             pltpu.VMEM((n_o, SUB, TILE), F32),
             pltpu.VMEM((n_o, SUB, TILE), F32),
             pltpu.SemaphoreType.DMA((LOAD,)),
-            pltpu.SemaphoreType.DMA((3 + 5 * ITERS,)),
-            pltpu.SemaphoreType.DMA((3 + 5 * ITERS,)),
+            pltpu.SemaphoreType.DMA((3 + 6 * ITERS,)),
+            pltpu.SemaphoreType.DMA((3 + 6 * ITERS,)),
             pltpu.SemaphoreType.DMA((n_f // 2,)),
             pltpu.SemaphoreType.DMA((n_f // 2,)),
             pltpu.SemaphoreType.DMA((ITERS, n_o)),
-            pltpu.SemaphoreType.DMA((ITERS, n_o)),
+            pltpu.SemaphoreType.DMA((ITERS, n_o * n_f // 2)),
+            pltpu.SemaphoreType.DMA((ITERS,)),
         ],
         compiler_params=pltpu.CompilerParams(
             collective_id=0, has_side_effects=True, vmem_limit_bytes=60 << 20
         ),
     )(slices, tile_brick[:, :, 0], tile_base, fluence[None, :], counts)
+    new, brick = pl.pallas_call(
+        hand_over,
+        out_shape=shapes,
+        in_specs=[vmem, vmem],
+        out_specs=(vmem, vmem),
+    )(*both)
     return new, brick.reshape(1, SUB * TILE)
 
 

time: 84.9 us -> 80.7 us (0.951)
  local copies, waits for them, and re-layouts: 2.65 us -> 0 us
  Pallas kernels: 81.4 us -> 79.8 us
    unnamed x2 -> x0, local copies, waits for them, and re-layouts: 2.65 us -> none
    pallas_call x1 -> x2, Pallas kernels: 81.4 us -> 79.8 us  [the longest x1 78.4 us: on_device(): pl.pallas_call(functools.partial(kernel, n_o, n_f), out_shape=shapes, in_...]
where the time goes in v5:
time: 80.7 us; the launch traced here: 80.5 us
  Pallas kernels  79.8 us (99%)
    pallas_call x1, Pallas kernels, on_device(): pl.pallas_call(functools.partial(kernel, n_o, n_f), out_shape=shapes, in_...  78.4 us

profile of v5, /device:TPU:1, one launch (start us, length us, event | category | flops | bytes accessed | tf_op | source)
XLA Modules:
  0.0 80.5 jit_solution(4474305209233029562)
XLA Ops:
  0.6 78.4 %shard_map.68 = (f32[64,128]{1,0:T(8,128)}, f32[8,128]{1,0:T(8,128)}) custom-call(f32[64,128]{1,0:T(8,128)} %slices_ref.1, s32[1,64]{1,0:T(1,128)} %bitcast.4, s32[1,64]{1,0:T(1,128)} %base_ref.1, f32[1,512]{1,0:T(1,128)} %bitcast.3, f32[512,2048]{1,0:T(8,128)} %counts_ref.1), custom_call_target="tpu_custom_call" | custom-call | tf_op jit(solution)/shard_map/pallas_call | solution.py:512
  79.1 1.4 %shard_map.69 = (f32[64,128]{1,0:T(8,128)}, f32[8,128]{1,0:T(8,128)}) custom-call(f32[64,128]{1,0:T(8,128)} %get-tuple-element.6.new_ref, f32[8,128]{1,0:T(8,128)} %get-tuple-element.7.brick_ref), custom_call_target="tpu_custom_call" | custom-call | tf_op jit(solution)/shard_map/pallas_call | solution.py:554

commit v6 on v5

--- a/solution.py
+++ b/solution.py
@@ -41,10 +41,14 @@
     slices_ref,
     brick_ref,
     base_ref,
-    fluence_ref,
+    fluence_from,
     counts_ref,
     new_ref,
     out_ref,
+    brick_here,
+    base_here,
+    fluence_ref,
+    totals,
     raw,
     count_high,
     count_low,
@@ -133,10 +137,19 @@
         return k in same_core or i == here_o or hops(i, k) >= far
 
     step = frames // LOAD
-    for i in range(LOAD):
-        pltpu.make_async_copy(
-            counts_ref.at[pl.ds(i * step, step)], raw.at[pl.ds(i * step, step)], load_sem.at[i]
-        ).start()
+    small = [
+        pltpu.make_async_copy(src, dst, load_sem.at[LOAD + i])
+        for i, (src, dst) in enumerate(
+            [
+                (brick_ref, brick_here),
+                (base_ref, base_here),
+                (fluence_from, fluence_ref),
+                (slices_ref, held.at[0, f, pl.ds(0, rows)]),
+            ]
+        )
+    ]
+    for one in small:
+        one.start()
     barrier = pltpu.get_barrier_semaphore()
     peers = [(i, k) for i in range(n_o) for k in range(n_f) if is_peer(i, k)]
     for i, k in sorted(peers, key=lambda d: -hops(*d)):
@@ -144,15 +157,21 @@
             barrier, inc=1, device_id=(peers_o[i], peers_f[k]), device_id_type=MESH
         )
 
-    held[0, f, 0:rows] = slices_ref[...]
-    named = brick_ref[...]
+    for i in range(LOAD):
+        pltpu.make_async_copy(
+            counts_ref.at[pl.ds(i * step, step)], raw.at[pl.ds(i * step, step)], load_sem.at[i]
+        ).start()
+    for one in small:
+        one.wait()
+
+    named = brick_here[...]
     inside = lax.rem(named, n_f)
     place = (
         lax.div(named, n_f) * block
         + (lax.rem(inside, 2) * half + lax.div(inside, 2)) * SUB
-        + lax.div(base_ref[...], TILE)
+        + lax.div(base_here[...], TILE)
     )
-    shift = lax.rem(base_ref[...], TILE)
+    shift = lax.rem(base_here[...], TILE)
     held[0, f, rows : rows + 1] = jnp.concatenate([place, place + 1], axis=1).astype(F32)
     held[0, f, rows + 1 : rows + 2] = jnp.concatenate([shift, shift], axis=1).astype(F32)
     held[0, f, rows + 2 : rows + SUB] = jnp.zeros((SUB - 2, TILE), F32)
@@ -166,8 +185,6 @@
             high, low = split2(raw[here, at])
             count_high[here, at] = high
             count_low[here, at] = low
-            count_high_t[at, here] = high.T
-            count_low_t[at, here] = low.T
             return c
 
         lax.fori_loop(0, n_f, convert, 0)
@@ -176,37 +193,37 @@
         load(i)
     pl.semaphore_wait(barrier, len(peers))
 
-    def copy(which, src, dst, to):
+    def copy(which, turn, src, dst, to):
         return pltpu.make_async_remote_copy(
             src_ref=src,
             dst_ref=dst,
             send_sem=send_sem.at[which],
-            recv_sem=recv_sem.at[which],
+            recv_sem=recv_sem.at[which, turn],
             device_id=to,
             device_id_type=MESH,
         )
 
-    def send_frame(which, src, dst):
+    def send_frame(which, turn, src, dst):
         def body(j, c):
             peer = lax.rem(f + j, n_f)
-            copy(which, src(peer), dst, (o, peer)).start()
+            copy(which, turn, src(peer), dst, (o, peer)).start()
             return c
 
         lax.fori_loop(1, n_f, body, 0)
 
-    def send_orient(which, src, dst):
+    def send_orient(which, turn, src, dst):
         def body(j, c):
             peer = lax.rem(o + j, n_o)
-            copy(which, src(peer), dst, (peer, f)).start()
+            copy(which, turn, src(peer), dst, (peer, f)).start()
             return c
 
         lax.fori_loop(1, n_o, body, 0)
 
-    def received(which, whole):
-        copy(which, whole, whole, (lax.rem(o + 1, n_o), f)).wait_recv()
+    def received(which, turn, whole):
+        copy(which, turn, whole, whole, (lax.rem(o + 1, n_o), f)).wait_recv()
 
     def sent(which, whole):
-        copy(which, whole, whole, (lax.rem(o + 1, n_o), f)).wait_send()
+        copy(which, 0, whole, whole, (lax.rem(o + 1, n_o), f)).wait_send()
 
     def deliver(src, dst, out, into, to):
         return pltpu.make_async_remote_copy(
@@ -218,24 +235,59 @@
             device_id_type=MESH,
         )
 
-    def pass_first(at):
+    def pass_first(at, distance):
         packet = held.at[0, at * 2 + core]
-        deliver(packet, packet, send_sem.at[1], first_pass.at[at], (o, sibling)).start()
-
-    away = [k for k in same_core if k != here_f]
+        deliver(packet, packet, send_sem.at[1], first_pass.at[distance], (o, sibling)).start()
+
+    def take(t, value):
+        at = pl.ds(t * TILE if isinstance(t, int) else pl.multiple_of(t * TILE, TILE), TILE)
+        high, mid, low = split3(jnp.log(value + BACKGROUND))
+        logs[0:rows, at] = high
+        logs[rows : 2 * rows, at] = mid
+        logs[2 * rows : 3 * rows, at] = low
+        return value
+
+    away = sorted(
+        (k for k in same_core if k != here_f), key=lambda k: -hops(here_o, k)
+    )
+    edge = hops(here_o, away[0])
+    packet = held.at[0, f]
     for k in away:
-        packet = held.at[0, f]
-        deliver(packet, packet, send_sem.at[0], first_recv.at[chip], (o, peers_f[k])).start()
-    pass_first(chip)
+        deliver(packet, packet, send_sem.at[0], first_recv.at[hops(here_o, k)], (o, peers_f[k])).start()
+        if hops(here_o, k) == edge:
+            across = (o, chips[k] * 2 + 1 - core)
+            deliver(packet, packet, send_sem.at[0], first_pass.at[edge], across).start()
+    pass_first(chip, 0)
+    def turn_over(j, c):
+        at = pl.ds(pl.multiple_of(j * TILE, TILE), TILE)
+        count_high_t[at, :] = count_high[:, at].T
+        count_low_t[at, :] = count_low[:, at].T
+        return c
+
+    lax.fori_loop(0, n_f, turn_over, 0)
+
+    for distance in range(1, edge + 1):
+        ring_of = [k for k in away if hops(here_o, k) == distance]
+        if ring_of:
+            some = held.at[0, pl.ds(0, len(ring_of))]
+            into = first_recv.at[distance]
+            deliver(some, some, send_sem.at[0], into, (o, sibling)).wait_recv()
+        if distance < edge:
+            for k in ring_of:
+                pass_first(chips[k], distance)
+    total = take(f, held[0, f, 0:rows])
     for k in reversed(away):
-        packet = held.at[0, peers_f[k]]
-        into = first_recv.at[chips[k]]
-        deliver(packet, packet, send_sem.at[0], into, (o, sibling)).wait_recv()
-        pass_first(chips[k])
-    for k in reversed(same_core):
-        packet = held.at[0, chips[k] * 2 + 1 - core]
-        into = first_pass.at[chips[k]]
-        deliver(packet, packet, send_sem.at[1], into, (o, sibling)).wait_recv()
+        total = total + take(peers_f[k], held[0, peers_f[k], 0:rows])
+    for distance in range(edge + 1):
+        ring_of = [k for k in same_core if hops(here_o, k) == distance]
+        if ring_of:
+            some = held.at[0, pl.ds(0, len(ring_of))]
+            into = first_pass.at[distance]
+            deliver(some, some, send_sem.at[1], into, (o, sibling)).wait_recv()
+        for k in ring_of:
+            at = chips[k] * 2 + 1 - core
+            total = total + take(at, held[0, at, 0:rows])
+    totals[...] = total
     diagonal = iota((rows, TILE), 0) == lane
     eye = iota((pair, pair), 0) == iota((pair, pair), 1)
 
@@ -280,7 +332,7 @@
         hits = jnp.dot(chosen, marks[...], preferred_element_type=F32)
         for i in range(n_o):
             hits_out[i] = hits[i * SUB : (i + 1) * SUB]
-        send_orient(2, lambda peer: hits_out.at[peer], hits_in.at[o])
+        send_orient(2, 0, lambda peer: hits_out.at[peer], hits_in.at[o])
         hits_in[o] = hits_out[o]
 
     def expand(t, many):
@@ -303,17 +355,7 @@
         return values
 
     def iteration(turn, c):
-        def take_logs(t, total):
-            value = held[turn, t, 0:rows]
-            at = pl.ds(pl.multiple_of(t * TILE, TILE), TILE)
-            high, mid, low = split3(jnp.log(value + BACKGROUND))
-            logs[0:rows, at] = high
-            logs[rows : 2 * rows, at] = mid
-            logs[2 * rows : 3 * rows, at] = low
-            return total + value
-
-        total = lax.fori_loop(0, n_f, take_logs, jnp.zeros((rows, TILE), F32))
-        total = jnp.sum(total, axis=1, keepdims=True)
+        total = jnp.sum(totals[...], axis=1, keepdims=True)
         like = jnp.dot(logs[...], count_high_t[...], preferred_element_type=F32) + jnp.dot(
             logs[...], count_low_t[...], preferred_element_type=F32
         )
@@ -326,14 +368,14 @@
         for k in range(chunks):
             own[k : k + 1, :] = top[:, k * TILE : (k + 1) * TILE]
             own[chunks + k : chunks + k + 1, :] = norm[:, k * TILE : (k + 1) * TILE]
-        send_orient(3 + turn, lambda peer: stats.at[turn, o], stats.at[turn, o])
+        send_orient(3, turn, lambda peer: stats.at[turn, o], stats.at[turn, o])
 
         @pl.when(turn == 0)
         def _():
             by_twos(prepare_to)
             count_hits()
 
-        received(3 + turn, stats.at[turn, pl.ds(0, n_o - 1)])
+        received(3, turn, stats.at[turn, pl.ds(0, n_o - 1)])
         peak = stats[turn, 0, 0:chunks, :]
         for i in range(1, n_o):
             peak = jnp.maximum(peak, stats[turn, i, 0:chunks, :])
@@ -347,7 +389,7 @@
         prob = expo * factor
         den = jnp.sum(prob * fluence_ref[...], axis=1, keepdims=True)
         dens[turn, f] = jnp.sum(jnp.where(diagonal, den, 0.0), axis=0, keepdims=True)
-        send_frame(5 + turn, lambda peer: dens.at[turn, f], dens.at[turn, f])
+        send_frame(4, turn, lambda peer: dens.at[turn, f], dens.at[turn, f])
 
         probs = jnp.concatenate(split2(prob), axis=0)
         num = jnp.dot(probs, count_high[...], preferred_element_type=F32) + jnp.dot(
@@ -365,7 +407,7 @@
         def _():
             by_twos(prepare_from)
 
-        received(5 + turn, dens.at[turn, pl.ds(0, n_f - 1)])
+        received(4, turn, dens.at[turn, pl.ds(0, n_f - 1)])
         weight = dens[turn, 0]
         for i in range(1, n_f):
             weight = weight + dens[turn, i]
@@ -395,24 +437,24 @@
                 deliver(
                     part_out.at[turn, 1 - core, i],
                     pair_in.at[turn, i],
-                    send_sem.at[13 + turn],
-                    pair_recv.at[turn, i],
+                    send_sem.at[8],
+                    pair_recv.at[turn, g],
                     (o, sibling),
                 ).start()
 
         def release(g):
+            got = pair_in.at[turn, pl.ds(g * group, group)]
+            into = pair_recv.at[turn, g]
+            deliver(got, got, send_sem.at[8], into, (o, sibling)).wait_recv()
             for i in range(g * group, (g + 1) * group):
-                into = pair_recv.at[turn, i]
-                got = pair_in.at[turn, i]
-                deliver(got, got, send_sem.at[13 + turn], into, (o, sibling)).wait_recv()
                 paired[turn, i] = part_out[turn, core, i] + pair_in[turn, i]
                 for k in same_core:
                     if (i, k) != (here_o, here_f):
                         deliver(
                             paired.at[turn, i, chips[k]],
                             part_in.at[turn, o * half + chip],
-                            send_sem.at[7 + turn],
-                            recv_sem.at[7 + turn],
+                            send_sem.at[5],
+                            recv_sem.at[5, turn],
                             (peers_o[i], peers_f[k]),
                         ).start()
 
@@ -426,10 +468,10 @@
 
         @pl.when(turn == 0)
         def _():
-            received(2, hits_in.at[pl.ds(0, n_o - 1)])
+            received(2, 0, hits_in.at[pl.ds(0, n_o - 1)])
 
         hits = jnp.sum(hits_in[...], axis=0)
-        received(7 + turn, part_in.at[turn, pl.ds(0, n // 2 - 1)])
+        received(5, turn, part_in.at[turn, pl.ds(0, n // 2 - 1)])
         brick = jnp.sum(part_in[turn], axis=0) / jnp.maximum(hits, 1.0)
         out_ref[...] = brick
         slot = o * n_f + mine
@@ -437,33 +479,35 @@
 
         for i, k in others:
             brick_at = volume.at[turn, slot]
-            into = wide_recv.at[turn, o * half + chip]
+            into = wide_recv.at[turn, hops(i, k)]
             deliver(
-                brick_at, brick_at, send_sem.at[9 + turn], into, (peers_o[i], peers_f[k])
+                brick_at, brick_at, send_sem.at[6], into, (peers_o[i], peers_f[k])
             ).start()
             if hops(i, k) >= far:
                 across = (peers_o[i], chips[k] * 2 + 1 - core)
                 deliver(
-                    brick_at, brick_at, send_sem.at[9 + turn], wide_pass.at[turn], across
+                    brick_at, brick_at, send_sem.at[6], wide_pass.at[turn], across
                 ).start()
 
         def pass_on(at):
             brick_at = volume.at[turn, at]
             deliver(
-                brick_at, brick_at, send_sem.at[11 + turn], wide_pass.at[turn], (o, sibling)
+                brick_at, brick_at, send_sem.at[7], wide_pass.at[turn], (o, sibling)
             ).start()
 
         pass_on(slot)
-        for i, k in reversed(others):
-            at = peers_o[i] * n_f + core * half + chips[k]
-            into = wide_recv.at[turn, peers_o[i] * half + chips[k]]
-            brick_at = volume.at[turn, at]
-            deliver(brick_at, brick_at, send_sem.at[9 + turn], into, (o, sibling)).wait_recv()
-            if hops(i, k) < far:
-                pass_on(at)
+        for distance in range(1, far + 2):
+            ring_of = [d for d in others if hops(*d) == distance]
+            if ring_of:
+                some = volume.at[turn, pl.ds(0, len(ring_of))]
+                into = wide_recv.at[turn, distance]
+                deliver(some, some, send_sem.at[6], into, (o, sibling)).wait_recv()
+            if distance < far:
+                for i, k in ring_of:
+                    pass_on(peers_o[i] * n_f + core * half + chips[k])
         bricks = volume.at[turn, pl.ds(0, n_o * half)]
         deliver(
-            bricks, bricks, send_sem.at[11 + turn], wide_pass.at[turn], (o, sibling)
+            bricks, bricks, send_sem.at[7], wide_pass.at[turn], (o, sibling)
         ).wait_recv()
         high, low = split2(volume[turn].reshape(places, TILE))
         spread[:, :TILE] = high
@@ -471,31 +515,29 @@
 
         @pl.when(turn < ITERS - 1)
         def _():
+            total = jnp.zeros((rows, TILE), F32)
             for t in range(0, n_f, 4):
                 for k, value in enumerate(expand(t, 4)):
                     held[turn + 1, t + k, 0:rows] = value
+                    total = total + take(t + k, value)
+            totals[...] = total
 
         return c
 
     lax.fori_loop(0, ITERS, iteration, 0)
     new_ref[...] = expand(f, 1)[0]
 
-    sent(0, held.at[0, pl.ds(0, half - 1)])
-    sent(1, held.at[0, pl.ds(0, half)])
+    edges = sum(hops(here_o, k) == edge for k in away)
+    sent(0, held.at[0, pl.ds(0, half - 1 + edges)])
+    sent(1, held.at[0, pl.ds(0, half - edges)])
     sent(2, hits_out.at[pl.ds(0, n_o - 1)])
-    for turn in range(ITERS):
-        sent(3 + turn, stats.at[turn, pl.ds(0, n_o - 1)])
-        sent(5 + turn, dens.at[turn, pl.ds(0, n_f - 1)])
-        sent(7 + turn, part_in.at[turn, pl.ds(0, n // 2 - 1)])
-        double = sum(hops(*d) >= far for d in others)
-        sent(9 + turn, volume.at[turn, pl.ds(0, n_o * half - 1 + double)])
-        sent(13 + turn, pair_in.at[turn])
-        sent(11 + turn, volume.at[turn, pl.ds(0, n_o * half - double)])
-
-
-def hand_over(new_ref, brick_ref, new_out, brick_out):
-    new_out[...] = new_ref[...]
-    brick_out[...] = brick_ref[...]
+    double = sum(hops(*d) >= far for d in others)
+    sent(3, stats.at[:, pl.ds(0, n_o - 1)])
+    sent(4, dens.at[:, pl.ds(0, n_f - 1)])
+    sent(5, part_in.at[:, pl.ds(0, n // 2 - 1)])
+    sent(6, volume.at[:, pl.ds(0, n_o * half - 1 + double)])
+    sent(7, volume.at[:, pl.ds(0, n_o * half - double)])
+    sent(8, pair_in)
 
 
 def on_device(n_o, n_f, slices, counts, fluence, tile_brick, tile_base):
@@ -505,16 +547,16 @@
     block = n_f * SUB
     places = n_o * block
     vmem = pl.BlockSpec(memory_space=pltpu.VMEM)
-    shapes = (
-        jax.ShapeDtypeStruct((rows, TILE), F32),
-        jax.ShapeDtypeStruct((SUB, TILE), F32),
-    )
-    both = pl.pallas_call(
+    new, brick = pl.pallas_call(
         functools.partial(kernel, n_o, n_f),
-        out_shape=shapes,
-        in_specs=[vmem, vmem, vmem, vmem, pl.BlockSpec(memory_space=pl.ANY)],
+        out_shape=(pltpu.VMEM((rows, TILE), F32), pltpu.VMEM((SUB, TILE), F32)),
+        in_specs=[pl.BlockSpec(memory_space=pl.ANY)] * 5,
         out_specs=(vmem, vmem),
         scratch_shapes=[
+            pltpu.VMEM((1, rows), jnp.int32),
+            pltpu.VMEM((1, rows), jnp.int32),
+            pltpu.VMEM((1, frames), F32),
+            pltpu.VMEM((rows, TILE), F32),
             pltpu.VMEM((frames, pixels), F32),
             pltpu.VMEM((frames, pixels), BF16),
             pltpu.VMEM((frames, pixels), BF16),
@@ -538,25 +580,19 @@
             pltpu.VMEM((places, 2 * TILE), BF16),
             pltpu.VMEM((n_o, SUB, TILE), F32),
             pltpu.VMEM((n_o, SUB, TILE), F32),
-            pltpu.SemaphoreType.DMA((LOAD,)),
-            pltpu.SemaphoreType.DMA((3 + 6 * ITERS,)),
-            pltpu.SemaphoreType.DMA((3 + 6 * ITERS,)),
-            pltpu.SemaphoreType.DMA((n_f // 2,)),
-            pltpu.SemaphoreType.DMA((n_f // 2,)),
-            pltpu.SemaphoreType.DMA((ITERS, n_o)),
-            pltpu.SemaphoreType.DMA((ITERS, n_o * n_f // 2)),
+            pltpu.SemaphoreType.DMA((LOAD + 4,)),
+            pltpu.SemaphoreType.DMA((9,)),
+            pltpu.SemaphoreType.DMA((6, ITERS)),
+            pltpu.SemaphoreType.DMA((5,)),
+            pltpu.SemaphoreType.DMA((5,)),
+            pltpu.SemaphoreType.DMA((ITERS, 4)),
+            pltpu.SemaphoreType.DMA((ITERS, 7)),
             pltpu.SemaphoreType.DMA((ITERS,)),
         ],
         compiler_params=pltpu.CompilerParams(
             collective_id=0, has_side_effects=True, vmem_limit_bytes=60 << 20
         ),
     )(slices, tile_brick[:, :, 0], tile_base, fluence[None, :], counts)
-    new, brick = pl.pallas_call(
-        hand_over,
-        out_shape=shapes,
-        in_specs=[vmem, vmem],
-        out_specs=(vmem, vmem),
-    )(*both)
     return new, brick.reshape(1, SUB * TILE)
 
 

time: 80.7 us -> 76.3 us (0.945)
  Pallas kernels: 79.8 us -> 74.3 us
  local copies, waits for them, and re-layouts: 0 us -> 1.21 us
    pallas_call x2 -> x1, Pallas kernels: 79.8 us -> 74.3 us  [on_device(): pl.pallas_call(functools.partial(kernel, n_o, n_f), out_shape=(pltpu.VMEM...]
    unnamed x0 -> x2, local copies, waits for them, and re-layouts: none -> 1.21 us
where the time goes in v6:
time: 76.3 us; the launch traced here: 76.1 us
  Pallas kernels  74.3 us (97%)
  local copies, waits for them, and re-layouts  1.21 us (2%)
    pallas_call x1, Pallas kernels, on_device(): pl.pallas_call(functools.partial(kernel, n_o, n_f), out_shape=(pltpu.VMEM...  74.3 us

profile of v6, /device:TPU:1, one launch (start us, length us, event | category | flops | bytes accessed | tf_op | source)
XLA Modules:
  0.0 76.1 jit_solution(12769690883944671173)
XLA Ops:
  0.6 74.3 %shard_map.68 = (f32[64,128]{1,0:T(8,128)S(1)}, f32[8,128]{1,0:T(8,128)S(1)}) custom-call(f32[64,128]{1,0:T(8,128)} %slices_ref.1, s32[1,64]{1,0:T(1,128)} %bitcast.5, s32[1,64]{1,0:T(1,128)} %base_ref.1, f32[1,512]{1,0:T(1,128)} %bitcast.4, f32[512,2048]{1,0:T(8,128)} %counts_ref.1), custom_call_target="tpu_custom_call" | custom-call | tf_op jit(solution)/shard_map/pallas_call | solution.py:550
  74.9 0.6 copy.9
  75.5 0.6 copy.10

commit v7 on v6

--- a/solution.py
+++ b/solution.py
@@ -17,6 +17,7 @@
 F32 = jnp.float32
 BF16 = jnp.bfloat16
 LOAD = 4
+FAR = 7
 
 
 def split2(x):
@@ -57,6 +58,7 @@
     held,
     stats,
     dens,
+    where_to,
     gather_to,
     gather_from,
     shifts,
@@ -131,6 +133,11 @@
     far = hops(*pairs[0]) - 1
     others = [d for d in pairs if d != (here_o, here_f)]
 
+    far_pairs = [d for d in pairs if hops(*d) >= far]
+    assert len(far_pairs) <= FAR
+    groups = 4
+    group = len(pairs) // groups
+
     def is_peer(i, k):
         if (i, k) == (here_o, here_f):
             return False
@@ -175,6 +182,15 @@
     held[0, f, rows : rows + 1] = jnp.concatenate([place, place + 1], axis=1).astype(F32)
     held[0, f, rows + 1 : rows + 2] = jnp.concatenate([shift, shift], axis=1).astype(F32)
     held[0, f, rows + 2 : rows + SUB] = jnp.zeros((SUB - 2, TILE), F32)
+
+    for g in range(groups):
+        for side in range(2):
+            for j in range(group):
+                i, k = pairs[g * group + j]
+                own_side = core if side == 0 else 1 - core
+                first = peers_o[i] * block + (own_side * half + chips[k]) * SUB
+                at = ((g * 2 + side) * group + j) * SUB
+                where_to[at : at + SUB, :] = (iota((SUB, pair), 0) + first).astype(F32)
 
     def load(i):
         here = pl.ds(i * step, step)
@@ -295,7 +311,7 @@
         row = held[0, t, rows : rows + 1]
         at = pl.ds(pl.multiple_of(t * pair, pair), pair)
         for i in range(n_o):
-            place = (iota((block, pair), 0) + peers_o[i] * block).astype(F32)
+            place = where_to[i * block : (i + 1) * block, :]
             gather_to[i * block : (i + 1) * block, at] = jnp.where(
                 place == row, 1.0, 0.0
             ).astype(BF16)
@@ -423,56 +439,63 @@
             tiles[at + rows : at + pair, :TILE] = jnp.where(first, none, high)
             tiles[at + rows : at + pair, TILE:] = jnp.where(first, none, low)
 
-        groups = min(4, n_o)
-        group = n_o // groups
+        def to_owner(src, at, to):
+            deliver(
+                src, part_in.at[turn, at], send_sem.at[5], recv_sem.at[5, turn], to
+            ).start()
 
         def product(g):
-            here = slice(g * group * block, (g + 1) * group * block)
+            here = slice(g * 2 * group * SUB, (g + 1) * 2 * group * SUB)
             part = jnp.dot(gather_to[here, :], tiles[...], preferred_element_type=F32)
-            part = (part[:, :TILE] + part[:, TILE:]).reshape(group, 2, half, SUB, TILE)
+            part = (part[:, :TILE] + part[:, TILE:]).reshape(2, group, SUB, TILE)
+            part_out[turn, g, 0] = part[0]
+            part_out[turn, g, 1] = part[1]
             for j in range(group):
-                i = g * group + j
-                for side in range(2):
-                    part_out[turn, side, i] = part[j, side]
-                deliver(
-                    part_out.at[turn, 1 - core, i],
-                    pair_in.at[turn, i],
-                    send_sem.at[8],
-                    pair_recv.at[turn, g],
-                    (o, sibling),
-                ).start()
+                i, k = pairs[g * group + j]
+                if hops(i, k) >= far:
+                    to_owner(
+                        part_out.at[turn, g, 0, j], o * half + chip, (peers_o[i], peers_f[k])
+                    )
+                    to_owner(
+                        part_out.at[turn, g, 1, j],
+                        n_o * half + far_pairs.index((i, k)),
+                        (peers_o[i], chips[k] * 2 + 1 - core),
+                    )
+            deliver(
+                part_out.at[turn, g, 1],
+                pair_in.at[turn, g],
+                send_sem.at[8],
+                pair_recv.at[turn, g],
+                (o, sibling),
+            ).start()
 
         def release(g):
-            got = pair_in.at[turn, pl.ds(g * group, group)]
+            got = pair_in.at[turn, g]
             into = pair_recv.at[turn, g]
             deliver(got, got, send_sem.at[8], into, (o, sibling)).wait_recv()
-            for i in range(g * group, (g + 1) * group):
-                paired[turn, i] = part_out[turn, core, i] + pair_in[turn, i]
-                for k in same_core:
-                    if (i, k) != (here_o, here_f):
-                        deliver(
-                            paired.at[turn, i, chips[k]],
-                            part_in.at[turn, o * half + chip],
-                            send_sem.at[5],
-                            recv_sem.at[5, turn],
-                            (peers_o[i], peers_f[k]),
-                        ).start()
+            paired[turn, g] = part_out[turn, g, 0] + pair_in[turn, g]
+            for j in range(group):
+                i, k = pairs[g * group + j]
+                if hops(i, k) < far and (i, k) != (here_o, here_f):
+                    to_owner(
+                        paired.at[turn, g, j], o * half + chip, (peers_o[i], peers_f[k])
+                    )
 
         for g in range(groups):
             product(g)
             if g >= 2:
                 release(g - 2)
-        for g in range(max(0, groups - 2), groups):
-            release(g)
-        part_in[turn, o * half + chip] = paired[turn, n_o - 1, chip]
+        release(groups - 2)
+        release(groups - 1)
+        part_in[turn, o * half + chip] = paired[turn, groups - 1, group - 1]
 
         @pl.when(turn == 0)
         def _():
             received(2, 0, hits_in.at[pl.ds(0, n_o - 1)])
 
         hits = jnp.sum(hits_in[...], axis=0)
-        received(5, turn, part_in.at[turn, pl.ds(0, n // 2 - 1)])
-        brick = jnp.sum(part_in[turn], axis=0) / jnp.maximum(hits, 1.0)
+        received(5, turn, part_in.at[turn, pl.ds(0, n // 2 - 1 + len(far_pairs))])
+        brick = jnp.sum(part_in[turn, 0 : n // 2 + len(far_pairs)], axis=0) / jnp.maximum(hits, 1.0)
         out_ref[...] = brick
         slot = o * n_f + mine
         volume[turn, slot] = brick
@@ -496,7 +519,7 @@
             ).start()
 
         pass_on(slot)
-        for distance in range(1, far + 2):
+        for distance in range(1, hops(*pairs[0]) + 1):
             ring_of = [d for d in others if hops(*d) == distance]
             if ring_of:
                 some = volume.at[turn, pl.ds(0, len(ring_of))]
@@ -531,10 +554,10 @@
     sent(0, held.at[0, pl.ds(0, half - 1 + edges)])
     sent(1, held.at[0, pl.ds(0, half - edges)])
     sent(2, hits_out.at[pl.ds(0, n_o - 1)])
-    double = sum(hops(*d) >= far for d in others)
+    double = len(far_pairs)
     sent(3, stats.at[:, pl.ds(0, n_o - 1)])
     sent(4, dens.at[:, pl.ds(0, n_f - 1)])
-    sent(5, part_in.at[:, pl.ds(0, n // 2 - 1)])
+    sent(5, part_in.at[:, pl.ds(0, n // 2 - 1 + double)])
     sent(6, volume.at[:, pl.ds(0, n_o * half - 1 + double)])
     sent(7, volume.at[:, pl.ds(0, n_o * half - double)])
     sent(8, pair_in)
@@ -565,6 +588,7 @@
             pltpu.VMEM((ITERS, n_f, rows + SUB, TILE), F32),
             pltpu.VMEM((ITERS, n_o, 2 * (frames // TILE), TILE), F32),
             pltpu.VMEM((ITERS, n_f, 1, TILE), F32),
+            pltpu.VMEM((places, pair), F32),
             pltpu.VMEM((places, n_f * pair), BF16),
             pltpu.VMEM((n_f * pair, places), BF16),
             pltpu.VMEM((n_f, rows, TILE), jnp.int32),
@@ -572,10 +596,10 @@
             pltpu.VMEM((n_f * pair, 2 * TILE), BF16),
             pltpu.VMEM((n_f * pair, TILE), BF16),
             pltpu.VMEM((3 * rows, pixels), BF16),
-            pltpu.VMEM((ITERS, 2, n_o, n_f // 2, SUB, TILE), F32),
-            pltpu.VMEM((ITERS, n_o, n_f // 2, SUB, TILE), F32),
-            pltpu.VMEM((ITERS, n_o, n_f // 2, SUB, TILE), F32),
-            pltpu.VMEM((ITERS, n_o * n_f // 2, SUB, TILE), F32),
+            pltpu.VMEM((ITERS, 4, 2, n_o * n_f // 8, SUB, TILE), F32),
+            pltpu.VMEM((ITERS, 4, n_o * n_f // 8, SUB, TILE), F32),
+            pltpu.VMEM((ITERS, 4, n_o * n_f // 8, SUB, TILE), F32),
+            pltpu.VMEM((ITERS, n_o * n_f // 2 + FAR, SUB, TILE), F32),
             pltpu.VMEM((ITERS, n_o * n_f, SUB, TILE), F32),
             pltpu.VMEM((places, 2 * TILE), BF16),
             pltpu.VMEM((n_o, SUB, TILE), F32),

time: 76.3 us -> 75.4 us (0.988)
  Pallas kernels: 74.3 us -> 73.4 us
    pallas_call x1, Pallas kernels: 74.3 us -> 73.4 us  [on_device(): pl.pallas_call(functools.partial(kernel, n_o, n_f), out_shape=(pltpu.VMEM...]
where the time goes in v7:
time: 75.4 us; the launch traced here: 75.3 us
  Pallas kernels  73.4 us (97%)
  local copies, waits for them, and re-layouts  1.21 us (2%)
    pallas_call x1, Pallas kernels, on_device(): pl.pallas_call(functools.partial(kernel, n_o, n_f), out_shape=(pltpu.VMEM...  73.4 us

profile of v7, /device:TPU:1, one launch (start us, length us, event | category | flops | bytes accessed | tf_op | source)
XLA Modules:
  0.0 75.3 jit_solution(9192580106089287006)
XLA Ops:
  0.6 73.4 %shard_map.68 = (f32[64,128]{1,0:T(8,128)S(1)}, f32[8,128]{1,0:T(8,128)S(1)}) custom-call(f32[64,128]{1,0:T(8,128)} %slices_ref.1, s32[1,64]{1,0:T(1,128)} %bitcast.5, s32[1,64]{1,0:T(1,128)} %base_ref.1, f32[1,512]{1,0:T(1,128)} %bitcast.4, f32[512,2048]{1,0:T(8,128)} %counts_ref.1), custom_call_target="tpu_custom_call" | custom-call | tf_op jit(solution)/shard_map/pallas_call | solution.py:573
  74.0 0.6 copy.9
  74.7 0.6 copy.10

commit v8 on v7

--- a/solution.py
+++ b/solution.py
@@ -130,7 +130,7 @@
     pairs = sorted(
         ((i, k) for i in range(n_o) for k in same_core), key=lambda d: -hops(*d)
     )
-    far = hops(*pairs[0]) - 1
+    far = hops(*pairs[0]) + 1
     others = [d for d in pairs if d != (here_o, here_f)]
 
     far_pairs = [d for d in pairs if hops(*d) >= far]
@@ -266,7 +266,7 @@
     away = sorted(
         (k for k in same_core if k != here_f), key=lambda k: -hops(here_o, k)
     )
-    edge = hops(here_o, away[0])
+    edge = hops(here_o, away[0]) + 1
     packet = held.at[0, f]
     for k in away:
         deliver(packet, packet, send_sem.at[0], first_recv.at[hops(here_o, k)], (o, peers_f[k])).start()

time: 75.4 us -> 72.7 us (0.964)
  Pallas kernels: 73.4 us -> 70.7 us
    pallas_call x1, Pallas kernels: 73.4 us -> 70.7 us  [on_device(): pl.pallas_call(functools.partial(kernel, n_o, n_f), out_shape=(pltpu.VMEM...]
where the time goes in v8:
time: 72.7 us; the launch traced here: 72.5 us
  Pallas kernels  70.7 us (97%)
  local copies, waits for them, and re-layouts  1.21 us (2%)
    pallas_call x1, Pallas kernels, on_device(): pl.pallas_call(functools.partial(kernel, n_o, n_f), out_shape=(pltpu.VMEM...  70.7 us

profile of v8, /device:TPU:1, one launch (start us, length us, event | category | flops | bytes accessed | tf_op | source)
XLA Modules:
  0.0 72.5 jit_solution(2785462261824929521)
XLA Ops:
  0.6 70.7 %shard_map.68 = (f32[64,128]{1,0:T(8,128)S(1)}, f32[8,128]{1,0:T(8,128)S(1)}) custom-call(f32[64,128]{1,0:T(8,128)} %slices_ref.1, s32[1,64]{1,0:T(1,128)} %bitcast.5, s32[1,64]{1,0:T(1,128)} %base_ref.1, f32[1,512]{1,0:T(1,128)} %bitcast.4, f32[512,2048]{1,0:T(8,128)} %counts_ref.1), custom_call_target="tpu_custom_call" | custom-call | tf_op jit(solution)/shard_map/pallas_call | solution.py:573
  71.3 0.6 copy.9
  72.0 0.6 copy.10

commit v9 on v8

--- a/solution.py
+++ b/solution.py
@@ -372,10 +372,12 @@
 
     def iteration(turn, c):
         total = jnp.sum(totals[...], axis=1, keepdims=True)
-        like = jnp.dot(logs[...], count_high_t[...], preferred_element_type=F32) + jnp.dot(
-            logs[...], count_low_t[...], preferred_element_type=F32
+        like = jnp.dot(logs[...], count_high_t[...], preferred_element_type=F32)
+        rest = jnp.dot(
+            logs[0 : 2 * rows, :], count_low_t[...], preferred_element_type=F32
         )
         like = like[:rows] + like[rows : 2 * rows] + like[2 * rows :]
+        like = like + (rest[:rows] + rest[rows:])
         score = SHARPNESS * (like - total * fluence_ref[...])
         top = jnp.max(score, axis=0, keepdims=True)
         expo = jnp.exp(score - top)
@@ -408,10 +410,10 @@
         send_frame(4, turn, lambda peer: dens.at[turn, f], dens.at[turn, f])
 
         probs = jnp.concatenate(split2(prob), axis=0)
-        num = jnp.dot(probs, count_high[...], preferred_element_type=F32) + jnp.dot(
-            probs, count_low[...], preferred_element_type=F32
-        )
-        num = num[:rows] + num[rows:]
+        num = jnp.dot(probs, count_high[...], preferred_element_type=F32)
+        num = (num[:rows] + num[rows:]) + jnp.dot(
+            probs[:rows], count_low[...], preferred_element_type=F32
+        )
         for t in range(n_f):
             value = num[:, t * TILE : (t + 1) * TILE] + jnp.where(f == t, held[turn, t, 0:rows], 0.0)
             shift = shifts[t]

time: 72.7 us -> 72.7 us (level)
  no operation moved by 1% of the time
where the time goes in v9:
time: 72.7 us; the launch traced here: 72.5 us
  Pallas kernels  70.6 us (97%)
  local copies, waits for them, and re-layouts  1.21 us (2%)
    pallas_call x1, Pallas kernels, on_device(): pl.pallas_call(functools.partial(kernel, n_o, n_f), out_shape=(pltpu.VMEM...  70.6 us

profile of v9, /device:TPU:1, one launch (start us, length us, event | category | flops | bytes accessed | tf_op | source)
XLA Modules:
  0.0 72.5 jit_solution(6390630051924789771)
XLA Ops:
  0.6 70.6 %shard_map.68 = (f32[64,128]{1,0:T(8,128)S(1)}, f32[8,128]{1,0:T(8,128)S(1)}) custom-call(f32[64,128]{1,0:T(8,128)} %slices_ref.1, s32[1,64]{1,0:T(1,128)} %bitcast.5, s32[1,64]{1,0:T(1,128)} %base_ref.1, f32[1,512]{1,0:T(1,128)} %bitcast.4, f32[512,2048]{1,0:T(8,128)} %counts_ref.1), custom_call_target="tpu_custom_call" | custom-call | tf_op jit(solution)/shard_map/pallas_call | solution.py:575
  71.3 0.6 copy.9
  71.9 0.6 copy.10
